TPU v7x, 32 devices: a whole 2x2x4 slice. The times are simulated.
32 devices in a mesh: groups: 2 (over y), seq: 4 (over z), segment: 2 (over x), owner: 2 (over core).
Axes of the slice: x: 2, y: 2, z: 4, core: 2. Of those that a mesh axis runs over, the one named last changes fastest.
Arguments:
- layer_input_rows: bfloat16 [2, 512, 5376], P('segment', ('groups', 'seq')), parts along dimension 1, may hold values from -40 to 40
- encoded_query_rows: bfloat16 [2, 512, 2048], P('segment', ('groups', 'seq'), 'owner'), parts along dimension 1, may hold values from -213 to 213
- encoded_key_rows: bfloat16 [2, 512, 1024], P('segment', ('groups', 'seq'), 'owner'), parts along dimension 1, may hold values from -6 to 6
- layer_norm_gain: float32 [2, 5376], P('segment'), may hold values from 0.25 to 1.75
- base_value_matrix: bfloat16 [2, 5376, 1024], P('segment', ('seq', 'owner')), may hold values from -0.078125 to 0.078125
- adapter_down_panels: bfloat16 [2, 8, 5376, 64], P('segment', 'seq', 'owner'), may hold values from -0.078125 to 0.078125
- adapter_up_panels: bfloat16 [2, 8, 64, 1024], P('segment', 'seq', None, 'owner'), may hold values from -0.75 to 0.75
- request_token_lengths: int32 [8], P('groups'), parts along dimension 0, may hold values from 1 to 128, 256 in all
- adapter_per_request: int32 [8], P('groups'), parts along dimension 0, may hold values from 0 to 7
- rank_per_adapter: int32 [8], replicated, may hold values from 16 to 64
- slot_per_adapter: int32 [8], replicated, may hold values from 0 to 7, each once
Outputs:
- layer_output: bfloat16 [2, 512, 2048], P('segment', ('groups', 'seq'), 'owner'), parts along dimension 1
There are 2 independent parts, one for each index of `groups`. A program takes and returns all parts, laid end to end along the dimension named above; an argument that names none is the same for every part. Nothing has to cross between parts.
All inputs are finite; a program needn't handle non-finite values.
Results may differ from a plain program's by a relative error of at most 0.0065.
Values may be sent and summed in bfloat16 or wider, within the bound.
A program may use at most 128 MiB of HBM per device.

v0:
```python
import functools

import jax
import jax.numpy as jnp
from jax import lax
from jax.experimental import pallas as pl
from jax.experimental.pallas import tpu as pltpu
from jax.sharding import PartitionSpec as P

WINDOW = 1024
HEADS = 16
KEY_VALUE_HEADS = 8
HEAD_SIZE = 128


query_scale = 168.0 ** (-0.5)
adapter_strength = 32.0
norm_eps = 1e-06


def broadcast(x, axis, root):
    mine = lax.axis_index(axis) == root
    return lax.psum(jnp.where(mine, x, jnp.zeros_like(x)), axis)


def from_behind(value, axis, steps):
    count = lax.axis_size(axis)
    first, last = (max(0, -steps), min(count, count - steps))
    return lax.ppermute(value, axis, [(source, source + steps) for source in range(first, last)])


def per_device(
    layer_input_rows,
    encoded_query_rows,
    encoded_key_rows,
    layer_norm_gain,
    base_value_matrix,
    adapter_down_panels,
    adapter_up_panels,
    request_token_lengths,
    adapter_per_request,
    rank_per_adapter,
    slot_per_adapter,
):
    hidden = layer_input_rows[0]
    row_count = hidden.shape[0]
    seq_now = lax.axis_index("seq")
    owner_now = lax.axis_index("owner")
    reach_count = min(WINDOW // row_count, lax.axis_size("seq") - 1)
    requests = request_token_lengths.shape[0]
    library = slot_per_adapter.shape[0]
    slots_here = adapter_down_panels.shape[1]
    rows_halved = adapter_down_panels.shape[2]
    rank_span_width = adapter_down_panels.shape[3]
    key_value_halved = adapter_up_panels.shape[3]
    group_size = HEADS // KEY_VALUE_HEADS
    request_ends = jnp.cumsum(request_token_lengths)
    position = seq_now * row_count + jnp.arange(row_count, dtype=jnp.int32)
    context = seq_now * row_count + jnp.arange(-reach_count * row_count, row_count, dtype=jnp.int32)
    request_lookup = jnp.sum((position[:, None] >= request_ends[None, :]).astype(jnp.int32), axis=1)
    request_ctx = jnp.sum((context[:, None] >= request_ends[None, :]).astype(jnp.int32), axis=1)
    live_mask = (context[None, :] <= position[:, None]) & (
        context[None, :] > position[:, None] - WINDOW
    )
    live_mask = (
        live_mask & (context[None, :] >= 0) & (request_ctx[None, :] == request_lookup[:, None])
    )
    choose = adapter_per_request[:, None] == jnp.arange(library, dtype=jnp.int32)[None, :]
    slot_of = jnp.sum(jnp.where(choose, slot_per_adapter[None, :], 0), axis=1)
    rank_lookup = jnp.sum(jnp.where(choose, rank_per_adapter[None, :], 0), axis=1)
    scale_lookup = adapter_strength / rank_lookup.astype(jnp.float32)
    in_request = request_lookup[:, None] == jnp.arange(requests, dtype=jnp.int32)[None, :]
    column_live = jnp.arange(rank_span_width, dtype=jnp.int32)[None, :] < rank_lookup[:, None]
    row_gain_weight = jnp.where(in_request, scale_lookup[None, :], jnp.float32(0.0))
    down_panel_here = adapter_down_panels[0]
    up_panel_here = adapter_up_panels[0]
    queries = encoded_query_rows[0]
    keys_own = encoded_key_rows[0]
    key_heads = keys_own.shape[1] // HEAD_SIZE
    wide_rows = hidden.astype(jnp.float32)
    normalized_rows = wide_rows * lax.rsqrt(
        jnp.mean(wide_rows * wide_rows, axis=1, keepdims=True) + norm_eps
    )
    normalized_rows = (normalized_rows * layer_norm_gain[0][None, :]).astype(jnp.bfloat16)
    normed_half = lax.dynamic_slice_in_dim(normalized_rows, owner_now * rows_halved, rows_halved, 1)
    full_value = jnp.dot(
        normalized_rows,
        lax.all_gather(base_value_matrix[0], ("seq", "owner"), axis=0, tiled=True),
        preferred_element_type=jnp.float32,
    )
    value_base_rows = lax.dynamic_slice_in_dim(
        full_value, owner_now * key_value_halved, key_value_halved, 1
    )

    def fetch_one(reduced_rows, request_index):
        owner_slot = slot_of[request_index]
        holder = owner_slot // slots_here
        local_slot = owner_slot % slots_here
        down_local = lax.dynamic_slice_in_dim(down_panel_here, local_slot, 1, 0)
        up_local = lax.dynamic_slice_in_dim(up_panel_here, local_slot, 1, 0)
        down_piece, up_piece = (
            broadcast(down_local, "seq", holder),
            broadcast(up_local, "seq", holder),
        )
        keep_mask = in_request[:, request_index][:, None] & column_live[request_index][None, :]
        matrix_product = jnp.dot(normed_half, down_piece[0], preferred_element_type=jnp.float32)
        return (reduced_rows + jnp.where(keep_mask, matrix_product, jnp.float32(0.0)), up_piece[0])

    start_low = jnp.zeros((row_count, rank_span_width), jnp.float32)
    reduced_rows, panels_up = lax.scan(fetch_one, start_low, jnp.arange(requests, dtype=jnp.int32))
    reduced_rows = lax.psum(reduced_rows, "owner").astype(jnp.bfloat16)
    raised_rows = jnp.einsum(
        "tr,qrk->qtk", reduced_rows, panels_up, preferred_element_type=jnp.float32
    )
    adapter_value = jnp.sum(row_gain_weight.T[:, :, None] * raised_rows, axis=0)
    value_output_rows = (value_base_rows + adapter_value).astype(jnp.bfloat16)
    key_parts = []
    value_parts = []
    for shift_by in range(reach_count, 0, -1):
        key_piece, value_piece = from_behind((keys_own, value_output_rows), "seq", shift_by)
        key_parts.append(key_piece)
        value_parts.append(value_piece)
    keys_all = jnp.concatenate(key_parts + [keys_own], axis=0)
    values_all = jnp.concatenate(value_parts + [value_output_rows], axis=0)
    query_view = queries.reshape(row_count, key_heads, group_size, HEAD_SIZE)
    key_view = keys_all.reshape(-1, key_heads, HEAD_SIZE)
    value_view = values_all.reshape(-1, key_heads, HEAD_SIZE)
    head_outputs = []
    for head_index in range(key_heads):
        query_head = query_view[:, head_index]
        scores = (
            jnp.einsum(
                "tcd,jd->ctj",
                query_head,
                key_view[:, head_index],
                preferred_element_type=jnp.float32,
            )
            * query_scale
        )
        scores = jnp.where(live_mask[None], scores, jnp.float32(-1e30))
        row_max = jnp.max(scores, axis=-1, keepdims=True)
        weights = jnp.exp(scores - row_max)
        row_total = jnp.sum(weights, axis=-1, keepdims=True)
        softmax_rows = (weights / row_total).astype(jnp.bfloat16)
        mixed = jnp.einsum(
            "ctj,jd->tcd",
            softmax_rows,
            value_view[:, head_index],
            preferred_element_type=jnp.float32,
        )
        head_outputs.append(mixed.astype(jnp.bfloat16).reshape(row_count, group_size * HEAD_SIZE))
    result = jnp.concatenate(head_outputs, axis=1)
    return result[None]


ROWS, LANES = 16, 128


def kernel(
    n,
    lengths,
    adapters,
    ranks,
    slots,
    x_hbm,
    q_hbm,
    k_hbm,
    gain_hbm,
    w_hbm,
    down_hbm,
    up_hbm,
    out_hbm,
    xs,
    xf,
    gain,
    wbuf,
    dn,
    dn_guest,
    lp_host,
    base,
    up,
    qb,
    kb,
    lp_mine,
    lp_other,
    part,
    vr,
    prob,
    ob,
    loc_sem,
    x_send_up,
    x_send_dn,
    x_recv,
    f_send,
    f_recv,
    w_send,
    w_recv,
    lp_send,
    lp_recv,
    q_send,
    q_recv,
    k_send,
    k_recv,
    rs_send,
    rs_recv,
    o_send,
    o_recv,
    p_send,
    p_recv,
    hk_send,
):
    f32, bf16 = jnp.float32, jnp.bfloat16
    s = lax.axis_index("seq")
    o = lax.axis_index("owner")
    tok, width = x_hbm.shape[1], x_hbm.shape[2]
    half = width // 2
    win = xf.shape[2]
    slab = w_hbm.shape[1]
    vcols = up.shape[2]
    panel_count, rank_width, _ = dn.shape
    head_cols = vcols // n
    q_cols = qb.shape[2]
    group = HEADS // KEY_VALUE_HEADS
    requests = lengths.shape[0]
    total = n * tok
    chip_rows = width // n
    per_half = n // 2

    def window(of):
        inside = (of % per_half) * chip_rows
        first = min(inside // LANES * LANES, half - win)
        return first, inside - first

    c = s // per_half
    place = lax.rem(s, per_half)
    first, pad = 0, 0
    for step in range(per_half):
        a, b = window(step)
        first = jnp.where(place == step, a, first)
        pad = jnp.where(place == step, b, pad)
    first = pl.multiple_of(first, LANES)
    other = 1 - o
    at_end = (s == 0) | (s == n - 1)
    guest = at_end & (o != c)
    keeper = at_end & (o == c)
    host_low, host_high = (s == 1) & (o == 1), (s == n - 2) & (o == 0)
    host = host_low | host_high
    end_of_host = jnp.where(host_low, 0, n - 1)
    host_seq = jnp.where(s == 0, 1, n - 2)
    can_up = (s < n - 1) & jnp.logical_not(host_high)
    can_down = (s > 0) & jnp.logical_not(host_low)

    def peer(seq, owner=None):
        return {"seq": seq, "owner": o if owner is None else owner}

    def remote(src, dst, send, recv, device):
        return pltpu.make_async_remote_copy(
            src_ref=src,
            dst_ref=dst,
            send_sem=send,
            recv_sem=recv,
            device_id=device,
            device_id_type=pl.DeviceIdType.MESH,
        )

    for step in range(per_half):
        _, b = window(step)

        @pl.when(place == step)
        def _():
            if b:
                wbuf[0:b, :] = jnp.zeros((b, vcols), bf16)
            rest = win - b - chip_rows
            if rest:
                wbuf[win - rest : win, :] = jnp.zeros((rest, vcols), bf16)

    barrier = pltpu.get_barrier_semaphore()
    for d in range(1, n):
        pl.semaphore_signal(
            barrier, inc=1, device_id=peer(lax.rem(s + d, n)), device_id_type=pl.DeviceIdType.MESH
        )
    pl.semaphore_signal(barrier, inc=1, device_id=peer(s, other), device_id_type=pl.DeviceIdType.MESH)

    @pl.when(host)
    def _():
        pl.semaphore_signal(
            barrier, inc=1, device_id=peer(end_of_host, other), device_id_type=pl.DeviceIdType.MESH
        )

    @pl.when(keeper)
    def _():
        pl.semaphore_signal(
            barrier, inc=1, device_id=peer(host_seq, other), device_id_type=pl.DeviceIdType.MESH
        )

    w_at = pl.ds(pl.multiple_of(pad + o * slab, ROWS), slab)
    my_cols = pl.ds(pl.multiple_of(o * vcols, LANES), vcols)
    other_cols = pl.ds(pl.multiple_of(other * vcols, LANES), vcols)
    my_half = pl.ds(pl.multiple_of(o * half, LANES), half)
    x_window = pl.ds(pl.multiple_of(c * half + first, LANES), win)
    my_head = pl.ds(pl.multiple_of(s * head_cols, LANES), head_cols)
    my_q = pl.ds(pl.multiple_of(s * q_cols, LANES), q_cols)
    local = [
        pltpu.make_async_copy(x_hbm.at[0, :, my_half], xs.at[s], loc_sem.at[0]),
        pltpu.make_async_copy(x_hbm.at[0, :, x_window], xf.at[s], loc_sem.at[1]),
        pltpu.make_async_copy(gain_hbm, gain, loc_sem.at[2]),
        pltpu.make_async_copy(down_hbm.at[0], dn, loc_sem.at[3]),
        pltpu.make_async_copy(up_hbm.at[0], up, loc_sem.at[4]),
        pltpu.make_async_copy(w_hbm.at[0, :, my_cols], wbuf.at[w_at], loc_sem.at[5]),
        pltpu.make_async_copy(q_hbm.at[0, :, my_q], qb.at[s], loc_sem.at[6]),
        pltpu.make_async_copy(k_hbm.at[0, :, my_head], kb.at[s], loc_sem.at[7]),
    ]
    for copy in local:
        copy.start()

    pl.semaphore_wait(barrier, n + (host | keeper).astype(jnp.int32))

    def x_copy(t, src, upward):
        to = s + 1 if upward else s - 1
        send = x_send_up if upward else x_send_dn
        return remote(src, xs.at[t], send.at[t], x_recv.at[t], peer(to))

    own_x = x_hbm.at[0, :, my_half]

    @pl.when(can_up)
    def _():
        x_copy(s, own_x, True).start()

    @pl.when(can_down)
    def _():
        x_copy(s, own_x, False).start()

    panel_copy = remote(down_hbm.at[0], dn_guest, p_send, p_recv, peer(host_seq))

    @pl.when(guest)
    def _():
        panel_copy.start()

    w_copy = remote(w_hbm.at[0, :, other_cols], wbuf.at[w_at], w_send, w_recv, peer(s, other))
    w_copy.start()

    def q_copy(to):
        cols = pl.ds(pl.multiple_of(to * q_cols, LANES), q_cols)
        return remote(q_hbm.at[0, :, cols], qb.at[s], q_send.at[to], q_recv.at[s], peer(to))

    def k_copy(to):
        cols = pl.ds(pl.multiple_of(to * head_cols, LANES), head_cols)
        return remote(k_hbm.at[0, :, cols], kb.at[s], k_send.at[to], k_recv.at[s], peer(to))

    ends, slot_of, rank_of = [], [], []
    run = jnp.int32(0)
    for r in range(requests):
        run = run + lengths[r]
        ends.append(run)
        adapter = adapters[r]
        slot_of.append(slots[adapter])
        rank_of.append(ranks[adapter])

    def request_at(position):
        found = jnp.zeros(position.shape, jnp.int32)
        for r in range(requests):
            found = found + (position >= ends[r]).astype(jnp.int32)
        return found

    for at in range(6):
        local[at].wait()

    def f_copy(t):
        return remote(
            xs.at[t, :, pl.ds(first, win)], xf.at[t], f_send.at[t], f_recv.at[t], peer(s, other)
        )

    def lp_copy(t):
        return remote(lp_mine.at[t], lp_other.at[t], lp_send.at[t], lp_recv.at[t], peer(s, other))

    def rs_copy(t, to):
        cols = pl.ds(pl.multiple_of(to * head_cols, LANES), head_cols)
        return remote(part.at[t, :, cols], vr.at[s, t], rs_send.at[t, to], rs_recv.at[s, t], peer(to))

    def host_copies(t):
        return (
            remote(lp_host.at[t], lp_other.at[t], hk_send.at[t], lp_recv.at[t], peer(end_of_host, other)),
        )

    def low_half(t, panels, result):
        rows = xs[t].astype(f32)
        scaled = (rows * gain[:, my_half]).astype(bf16)
        square = jnp.sum(rows * rows, axis=1, keepdims=True)
        product = lax.dot_general(
            scaled,
            panels[...].reshape(panel_count * rank_width, half),
            (((1,), (1,)), ((), ())),
            preferred_element_type=f32,
        )
        result[t, :, : panel_count * rank_width] = product
        result[t, :, panel_count * rank_width :] = jnp.broadcast_to(square, (tok, LANES))

    @pl.when(guest)
    def _():
        lp_mine[...] = jnp.zeros(lp_mine.shape, f32)

    def low_part(t):
        @pl.when(jnp.logical_not(guest))
        def _():
            low_half(t, dn, lp_mine)

        @pl.when(jnp.logical_not(at_end))
        def _():
            lp_copy(t).start()


    def base_part(t):
        scaled = (xf[t].astype(f32) * gain[:, x_window]).astype(bf16)
        base[t] = jnp.dot(scaled, wbuf[...], preferred_element_type=f32)

    def value_part(t):
        lp_copy(t).wait_recv()

        @pl.when(keeper)
        def _():
            lp_host[t] = lp_mine[t] + lp_other[t]
            remote(
                lp_host.at[t], lp_other.at[t], lp_send.at[t], lp_recv.at[t], peer(s, other)
            ).start()

        low_width = panel_count * rank_width
        square = lp_mine[t, :, low_width : low_width + 1] + lp_other[t, :, low_width : low_width + 1]
        inv = lax.rsqrt(square / width + norm_eps)
        low = (lp_mine[t, :, :low_width] + lp_other[t, :, :low_width]) * inv
        req = request_at(t * tok + lax.broadcasted_iota(jnp.int32, (tok, 1), 0))
        slot_t = jnp.zeros((tok, 1), jnp.int32)
        rank_t = jnp.ones((tok, 1), jnp.int32)
        for r in range(requests):
            slot_t = jnp.where(req == r, slot_of[r], slot_t)
            rank_t = jnp.where(req == r, rank_of[r], rank_t)
        column = lax.broadcasted_iota(jnp.int32, (tok, low_width), 1)
        begin = (slot_t - s * panel_count) * rank_width
        low = jnp.where((column >= begin) & (column < begin + rank_t), low, 0.0).astype(bf16)
        raised = jnp.dot(low, up[...].reshape(low_width, vcols), preferred_element_type=f32)
        scale = adapter_strength / rank_t.astype(f32)
        part[t] = (base[t] * inv + raised * scale).astype(bf16)
        for d in range(1, n):
            rs_copy(t, lax.rem(s + d, n)).start()
        vr[s, t] = part[t, :, my_head]

    low_part(s)

    def attention():
        local[6].wait()
        local[7].wait()
        for d in range(1, n):
            frm = lax.rem(s + n - d, n)
            remote(qb.at[frm], qb.at[frm], q_send.at[frm], q_recv.at[frm], peer(frm)).wait_recv()
            remote(kb.at[frm], kb.at[frm], k_send.at[frm], k_recv.at[frm], peer(frm)).wait_recv()
        keys = kb[...].reshape(total, head_cols)
        key_at = lax.broadcasted_iota(jnp.int32, (1, total), 1)
        key_req = request_at(key_at)
        for t in range(n):
            query_at = t * tok + lax.broadcasted_iota(jnp.int32, (tok, 1), 0)
            live = (key_at <= query_at) & (key_at > query_at - WINDOW)
            live = live & (request_at(query_at) == key_req)
            for h in range(q_cols // HEAD_SIZE):
                query = qb[t, :, h * HEAD_SIZE : (h + 1) * HEAD_SIZE]
                kv = h // group
                scores = (
                    lax.dot_general(
                        query,
                        keys[:, kv * HEAD_SIZE : (kv + 1) * HEAD_SIZE],
                        (((1,), (1,)), ((), ())),
                        preferred_element_type=f32,
                    )
                    * query_scale
                )
                scores = jnp.where(live, scores, -1e30)
                weights = jnp.exp(scores - jnp.max(scores, axis=1, keepdims=True))
                soft = weights / jnp.sum(weights, axis=1, keepdims=True)
                prob[h, t * tok : (t + 1) * tok, :] = soft.astype(bf16)

    for d in range(1, n):
        if d == n - 1:

            @pl.when(at_end)
            def _():
                def one(e, carry):
                    value_part(jnp.where(s == 0, e, n - 1 - e))
                    return carry

                lax.fori_loop(0, n - 1, one, 0)

        def arrive(below):
            t = s - d if below else s + d

            @pl.when(((t >= 0) if below else (t < n)) & jnp.logical_not(guest))
            def _():
                x_copy(t, xs.at[t], below).wait_recv()

                @pl.when(can_up if below else can_down)
                def _():
                    x_copy(t, xs.at[t], below).start()

                @pl.when(o == c)
                def _():
                    f_copy(t).start()
                    xf[t] = xs[t, :, pl.ds(first, win)]

        arrive(True)
        arrive(False)

        if d == n - 2:
            for e in range(1, n):
                to = lax.rem(s + e, n)
                q_copy(to).start()
                k_copy(to).start()

        if d == 1:
            w_copy.wait_recv()
            base_part(s)

            @pl.when(jnp.logical_not(at_end))
            def _():
                value_part(s)

        if d == n - 2:

            @pl.when(host)
            def _():
                panel_copy.wait_recv()

                def one(t, carry):
                    low_half(t, dn_guest, lp_host)
                    for copy in host_copies(t):
                        copy.start()
                    return carry

                lax.fori_loop(0, n, one, 0)

        def both(side, carry):
            t = s - d + 2 * d * side

            @pl.when((t >= 0) & (t < n))
            def _():
                low_part(t)

                @pl.when(o != c)
                def _():
                    f_copy(t).wait_recv()

                base_part(t)

                @pl.when(jnp.logical_not(at_end) | (d == n - 1))
                def _():
                    value_part(t)

            return carry

        lax.fori_loop(0, 2, both, 0)

    attention()

    for d in range(1, n):
        frm = lax.rem(s + d, n)
        for t in range(n):
            remote(vr.at[frm, t], vr.at[frm, t], rs_send.at[t, frm], rs_recv.at[frm, t], peer(frm)).wait_recv()
    values = vr[0].astype(f32)
    for frm in range(1, n):
        values = values + vr[frm].astype(f32)
    values = values.reshape(total, head_cols).astype(bf16)

    def o_copy(t):
        return remote(ob.at[t], out_hbm.at[0, :, my_q], o_send.at[t], o_recv.at[s], peer(t))

    for h in range(q_cols // HEAD_SIZE):
        kv = h // group
        mixed = jnp.dot(
            prob[h], values[:, kv * HEAD_SIZE : (kv + 1) * HEAD_SIZE], preferred_element_type=f32
        ).astype(bf16)
        ob[:, :, h * HEAD_SIZE : (h + 1) * HEAD_SIZE] = mixed.reshape(n, tok, HEAD_SIZE)
    for d in range(1, n):
        o_copy(lax.rem(s + d, n)).start()
    mine = pltpu.make_async_copy(ob.at[s], out_hbm.at[0, :, my_q], loc_sem.at[8])
    mine.start()

    w_copy.wait_send()

    @pl.when(guest)
    def _():
        panel_copy.wait_send()

    for d in range(1, n):
        to = lax.rem(s + d, n)
        q_copy(to).wait_send()
        k_copy(to).wait_send()
        for t in range(n):
            rs_copy(t, to).wait_send()
    for t in range(n):

        @pl.when(jnp.logical_not(guest))
        def _():
            lp_copy(t).wait_send()

        @pl.when(host)
        def _():
            for copy in host_copies(t):
                copy.wait_send()

        @pl.when((t <= s) & can_up)
        def _():
            x_copy(t, xs.at[t], True).wait_send()

        @pl.when((t >= s) & can_down)
        def _():
            x_copy(t, xs.at[t], False).wait_send()

        @pl.when((o == c) & (t != s))
        def _():
            f_copy(t).wait_send()

    mine.wait()
    for d in range(1, n):
        frm = lax.rem(s + d, n)
        o_copy(frm).wait_send()
        cols = pl.ds(pl.multiple_of(frm * q_cols, LANES), q_cols)
        remote(ob.at[frm], out_hbm.at[0, :, cols], o_send.at[frm], o_recv.at[frm], peer(frm)).wait_recv()


def fused(
    n,
    layer_input_rows,
    encoded_query_rows,
    encoded_key_rows,
    layer_norm_gain,
    base_value_matrix,
    adapter_down_panels,
    adapter_up_panels,
    request_token_lengths,
    adapter_per_request,
    rank_per_adapter,
    slot_per_adapter,
):
    f32, bf16 = jnp.float32, jnp.bfloat16
    tok, width = layer_input_rows.shape[1:]
    half = width // 2
    panels, _, rank_width = adapter_down_panels.shape[1:]
    vcols = adapter_up_panels.shape[3]
    qcols = encoded_query_rows.shape[2]
    chip_rows = width // n
    pads = [(i * chip_rows) % LANES for i in range(n // 2)]
    win = -(-(max(pads) + chip_rows) // LANES) * LANES
    total = n * tok
    low = panels * rank_width
    dma = pltpu.SemaphoreType.DMA
    any_spec = pl.BlockSpec(memory_space=pl.ANY)
    smem = pl.BlockSpec(memory_space=pltpu.SMEM)
    return pl.pallas_call(
        functools.partial(kernel, n),
        out_shape=jax.ShapeDtypeStruct(encoded_query_rows.shape, bf16),
        in_specs=[smem] * 4 + [any_spec] * 7,
        out_specs=any_spec,
        scratch_shapes=[
            pltpu.VMEM((n, tok, half), bf16),
            pltpu.VMEM((n, tok, win), bf16),
            pltpu.VMEM((1, width), f32),
            pltpu.VMEM((win, vcols), bf16),
            pltpu.VMEM((panels, rank_width, half), bf16),
            pltpu.VMEM((panels, rank_width, half), bf16),
            pltpu.VMEM((n, tok, low + LANES), f32),
            pltpu.VMEM((n, tok, vcols), f32),
            pltpu.VMEM((panels, rank_width, vcols), bf16),
            pltpu.VMEM((n, tok, qcols // n), bf16),
            pltpu.VMEM((n, tok, vcols // n), bf16),
            pltpu.VMEM((n, tok, low + LANES), f32),
            pltpu.VMEM((n, tok, low + LANES), f32),
            pltpu.VMEM((n, tok, vcols), bf16),
            pltpu.VMEM((n, n, tok, vcols // n), bf16),
            pltpu.VMEM((qcols // n // HEAD_SIZE, total, total), bf16),
            pltpu.VMEM((n, tok, qcols // n), bf16),
            dma((9,)),
            dma((n,)),
            dma((n,)),
            dma((n,)),
            dma((n,)),
            dma((n,)),
            dma,
            dma,
            dma((n,)),
            dma((n,)),
            dma((n,)),
            dma((n,)),
            dma((n,)),
            dma((n,)),
            dma((n, n)),
            dma((n, n)),
            dma((n,)),
            dma((n,)),
            dma,
            dma,
            dma((n,)),
        ],
        compiler_params=pltpu.CompilerParams(
            collective_id=0, has_side_effects=True, vmem_limit_bytes=56 * 1024 * 1024
        ),
    )(
        request_token_lengths,
        adapter_per_request,
        rank_per_adapter,
        slot_per_adapter,
        layer_input_rows,
        encoded_query_rows,
        encoded_key_rows,
        layer_norm_gain,
        base_value_matrix,
        jnp.swapaxes(adapter_down_panels, 2, 3),
        adapter_up_panels,
    )


def solution(mesh):
    in_specs = (
        P("segment", ("groups", "seq"), None),
        P("segment", ("groups", "seq"), "owner"),
        P("segment", ("groups", "seq"), "owner"),
        P("segment", None),
        P("segment", ("seq", "owner"), None),
        P("segment", "seq", "owner", None),
        P("segment", "seq", None, "owner"),
        P("groups"),
        P("groups"),
        P(),
        P(),
    )
    out_specs = P("segment", ("groups", "seq"), "owner")
    n = mesh.shape["seq"]
    key_heads = KEY_VALUE_HEADS // mesh.shape["owner"]
    small = mesh.shape["owner"] == 2 and n % 4 == 0 and key_heads % n == 0
    return jax.shard_map(
        functools.partial(fused, n) if small else per_device, mesh=mesh, in_specs=in_specs, out_specs=out_specs, check_vma=False
    )
```

profile of v0, /device:TPU:0, one launch (start us, length us, event | category | flops | bytes accessed | tf_op | source)
XLA Modules:
  0.0 47.2 jit_solution(12749461980333589224)
XLA Ops:
  0.0 45.6 %shard_map.109 = bf16[1,64,1024]{2,1,0:T(8,128)(2,1)} custom-call(s32[4]{0:T(128)} %lengths.1, s32[4]{0:T(128)} %adapters.1, s32[8]{0:T(128)} %ranks.1, s32[8]{0:T(128)} %slots.1, bf16[1,64,5376]{2,1,0:T(8,128)(2,1)} %x_hbm.1, bf16[1,64,1024]{2,1,0:T(8,128)(2,1)} %q_hbm.1, bf16[1,64,512]{2,1,0:T(8,128)(2,1)} %k_hbm.1, f32[1,5376]{1,0:T(1,128)} %gain_hbm.1, ...), custom_call_target="tpu_custom_call" | custom-call | tf_op jit(solution)/shard_map/pallas_call | solution.py:654
  45.6 1.6 %copy.13 = bf16[1,64,1024]{2,1,0:T(8,128)(2,1)} copy(bf16[1,64,1024]{2,1,0:T(8,128)(2,1)} %shard_map.109) | data formatting | bytes 262144
where the time goes:
time: 47.3 us; the launch traced here: 47.2 us
  Pallas kernels  45.6 us (96%)
  local copies, waits for them, and re-layouts  1.57 us (3%)
    pallas_call x1, Pallas kernels, fused(): pl.pallas_call(functools.partial(kernel, n), out_shape=jax.ShapeDtypeStru...  45.6 us
    unnamed x1, local copies, waits for them, and re-layouts  1.57 us

commit v1 on v0

v1 whole, which is shorter than its diff:
```python
import functools

import jax
import jax.numpy as jnp
from jax import lax
from jax.experimental import pallas as pl
from jax.experimental.pallas import tpu as pltpu
from jax.sharding import PartitionSpec as P

WINDOW = 1024
HEADS = 16
KEY_VALUE_HEADS = 8
HEAD_SIZE = 128


query_scale = 168.0 ** (-0.5)
adapter_strength = 32.0
norm_eps = 1e-06


def broadcast(x, axis, root):
    mine = lax.axis_index(axis) == root
    return lax.psum(jnp.where(mine, x, jnp.zeros_like(x)), axis)


def from_behind(value, axis, steps):
    count = lax.axis_size(axis)
    first, last = (max(0, -steps), min(count, count - steps))
    return lax.ppermute(value, axis, [(source, source + steps) for source in range(first, last)])


def per_device(
    layer_input_rows,
    encoded_query_rows,
    encoded_key_rows,
    layer_norm_gain,
    base_value_matrix,
    adapter_down_panels,
    adapter_up_panels,
    request_token_lengths,
    adapter_per_request,
    rank_per_adapter,
    slot_per_adapter,
):
    hidden = layer_input_rows[0]
    row_count = hidden.shape[0]
    seq_now = lax.axis_index("seq")
    owner_now = lax.axis_index("owner")
    reach_count = min(WINDOW // row_count, lax.axis_size("seq") - 1)
    requests = request_token_lengths.shape[0]
    library = slot_per_adapter.shape[0]
    slots_here = adapter_down_panels.shape[1]
    rows_halved = adapter_down_panels.shape[2]
    rank_span_width = adapter_down_panels.shape[3]
    key_value_halved = adapter_up_panels.shape[3]
    group_size = HEADS // KEY_VALUE_HEADS
    request_ends = jnp.cumsum(request_token_lengths)
    position = seq_now * row_count + jnp.arange(row_count, dtype=jnp.int32)
    context = seq_now * row_count + jnp.arange(-reach_count * row_count, row_count, dtype=jnp.int32)
    request_lookup = jnp.sum((position[:, None] >= request_ends[None, :]).astype(jnp.int32), axis=1)
    request_ctx = jnp.sum((context[:, None] >= request_ends[None, :]).astype(jnp.int32), axis=1)
    live_mask = (context[None, :] <= position[:, None]) & (
        context[None, :] > position[:, None] - WINDOW
    )
    live_mask = (
        live_mask & (context[None, :] >= 0) & (request_ctx[None, :] == request_lookup[:, None])
    )
    choose = adapter_per_request[:, None] == jnp.arange(library, dtype=jnp.int32)[None, :]
    slot_of = jnp.sum(jnp.where(choose, slot_per_adapter[None, :], 0), axis=1)
    rank_lookup = jnp.sum(jnp.where(choose, rank_per_adapter[None, :], 0), axis=1)
    scale_lookup = adapter_strength / rank_lookup.astype(jnp.float32)
    in_request = request_lookup[:, None] == jnp.arange(requests, dtype=jnp.int32)[None, :]
    column_live = jnp.arange(rank_span_width, dtype=jnp.int32)[None, :] < rank_lookup[:, None]
    row_gain_weight = jnp.where(in_request, scale_lookup[None, :], jnp.float32(0.0))
    down_panel_here = adapter_down_panels[0]
    up_panel_here = adapter_up_panels[0]
    queries = encoded_query_rows[0]
    keys_own = encoded_key_rows[0]
    key_heads = keys_own.shape[1] // HEAD_SIZE
    wide_rows = hidden.astype(jnp.float32)
    normalized_rows = wide_rows * lax.rsqrt(
        jnp.mean(wide_rows * wide_rows, axis=1, keepdims=True) + norm_eps
    )
    normalized_rows = (normalized_rows * layer_norm_gain[0][None, :]).astype(jnp.bfloat16)
    normed_half = lax.dynamic_slice_in_dim(normalized_rows, owner_now * rows_halved, rows_halved, 1)
    full_value = jnp.dot(
        normalized_rows,
        lax.all_gather(base_value_matrix[0], ("seq", "owner"), axis=0, tiled=True),
        preferred_element_type=jnp.float32,
    )
    value_base_rows = lax.dynamic_slice_in_dim(
        full_value, owner_now * key_value_halved, key_value_halved, 1
    )

    def fetch_one(reduced_rows, request_index):
        owner_slot = slot_of[request_index]
        holder = owner_slot // slots_here
        local_slot = owner_slot % slots_here
        down_local = lax.dynamic_slice_in_dim(down_panel_here, local_slot, 1, 0)
        up_local = lax.dynamic_slice_in_dim(up_panel_here, local_slot, 1, 0)
        down_piece, up_piece = (
            broadcast(down_local, "seq", holder),
            broadcast(up_local, "seq", holder),
        )
        keep_mask = in_request[:, request_index][:, None] & column_live[request_index][None, :]
        matrix_product = jnp.dot(normed_half, down_piece[0], preferred_element_type=jnp.float32)
        return (reduced_rows + jnp.where(keep_mask, matrix_product, jnp.float32(0.0)), up_piece[0])

    start_low = jnp.zeros((row_count, rank_span_width), jnp.float32)
    reduced_rows, panels_up = lax.scan(fetch_one, start_low, jnp.arange(requests, dtype=jnp.int32))
    reduced_rows = lax.psum(reduced_rows, "owner").astype(jnp.bfloat16)
    raised_rows = jnp.einsum(
        "tr,qrk->qtk", reduced_rows, panels_up, preferred_element_type=jnp.float32
    )
    adapter_value = jnp.sum(row_gain_weight.T[:, :, None] * raised_rows, axis=0)
    value_output_rows = (value_base_rows + adapter_value).astype(jnp.bfloat16)
    key_parts = []
    value_parts = []
    for shift_by in range(reach_count, 0, -1):
        key_piece, value_piece = from_behind((keys_own, value_output_rows), "seq", shift_by)
        key_parts.append(key_piece)
        value_parts.append(value_piece)
    keys_all = jnp.concatenate(key_parts + [keys_own], axis=0)
    values_all = jnp.concatenate(value_parts + [value_output_rows], axis=0)
    query_view = queries.reshape(row_count, key_heads, group_size, HEAD_SIZE)
    key_view = keys_all.reshape(-1, key_heads, HEAD_SIZE)
    value_view = values_all.reshape(-1, key_heads, HEAD_SIZE)
    head_outputs = []
    for head_index in range(key_heads):
        query_head = query_view[:, head_index]
        scores = (
            jnp.einsum(
                "tcd,jd->ctj",
                query_head,
                key_view[:, head_index],
                preferred_element_type=jnp.float32,
            )
            * query_scale
        )
        scores = jnp.where(live_mask[None], scores, jnp.float32(-1e30))
        row_max = jnp.max(scores, axis=-1, keepdims=True)
        weights = jnp.exp(scores - row_max)
        row_total = jnp.sum(weights, axis=-1, keepdims=True)
        softmax_rows = (weights / row_total).astype(jnp.bfloat16)
        mixed = jnp.einsum(
            "ctj,jd->tcd",
            softmax_rows,
            value_view[:, head_index],
            preferred_element_type=jnp.float32,
        )
        head_outputs.append(mixed.astype(jnp.bfloat16).reshape(row_count, group_size * HEAD_SIZE))
    result = jnp.concatenate(head_outputs, axis=1)
    return result[None]


LANES = 128
CHUNKS = 4


def kernel(
    n,
    lengths,
    adapters,
    ranks,
    slots,
    x_hbm,
    q_hbm,
    k_hbm,
    gain_hbm,
    w_hbm,
    down_hbm,
    up_hbm,
    out_hbm,
    xr,
    gain,
    xb,
    wbuf,
    dn,
    hdn,
    ucat,
    qb,
    kb,
    pown,
    pbuf,
    prec,
    sbuf,
    srec,
    vbuf,
    vall,
    prob,
    ob,
    loc_sem,
    xi_send,
    xo_send,
    x_recv,
    ex_send,
    ex_recv,
    ph_send,
    ph_recv,
    uh_send,
    uh_recv,
    k_send,
    k_recv,
    p_send,
    p_recv,
    s_send,
    s_recv,
    v_send,
    vc_send,
    v_recv,
):
    f32, bf16 = jnp.float32, jnp.bfloat16
    s = lax.axis_index("seq")
    o = lax.axis_index("owner")
    g = lax.axis_index("groups")
    tok, width = x_hbm.shape[1], x_hbm.shape[2]
    part = tok // 2
    half = width // 2
    win, vcols2 = wbuf.shape
    vcols = vcols2 // 2
    slab = w_hbm.shape[1]
    panels, rank_width = dn.shape[0], dn.shape[1]
    low_width = panels * rank_width
    chip_rows = width // n
    requests = lengths.shape[0]
    total = n * tok
    group = HEADS // KEY_VALUE_HEADS
    wide = -(-half // (2 * LANES)) * LANES
    sizes = (wide, half - wide)

    low_side = s < n // 2
    end = (s == 0) | (s == n - 1)
    inner = jnp.logical_not(end)
    near_end = jnp.where(low_side, 0, n - 1)
    near_inner = jnp.where(low_side, 1, n - 2)
    far_inner = n - 1 - near_inner
    far_end = n - 1 - near_end
    inward = low_side.astype(jnp.int32)
    outward = 1 - inward
    other = 1 - o
    host_core = inward

    def peer(seq, owner=None, groups=None):
        return {
            "seq": seq,
            "owner": o if owner is None else owner,
            "groups": g if groups is None else groups,
        }

    def remote(src, dst, send, recv, device):
        return pltpu.make_async_remote_copy(
            src_ref=src,
            dst_ref=dst,
            send_sem=send,
            recv_sem=recv,
            device_id=device,
            device_id_type=pl.DeviceIdType.MESH,
        )

    barrier = pltpu.get_barrier_semaphore()

    def greet(device):
        pl.semaphore_signal(barrier, inc=1, device_id=device, device_id_type=pl.DeviceIdType.MESH)

    greet(peer(s, other))

    @pl.when(end)
    def _():
        greet(peer(near_inner))
        greet(peer(near_inner, other))

    @pl.when(inner)
    def _():
        greet(peer(near_end))
        greet(peer(near_end, other))
        greet(peer(far_inner))
        greet(peer(s, o, 1 - g))

    begin = s * chip_rows
    first, pad = 0, 0
    for step in range(n):
        a = min(step * chip_rows // LANES * LANES, width - win)
        first = jnp.where(s == step, a, first)
        pad = jnp.where(s == step, step * chip_rows - a, pad)
    first = pl.multiple_of(first, LANES)
    x_window = pl.ds(first, win)
    w_at = pl.ds(pl.multiple_of(pad + o * slab, 16), slab)
    my_half = pl.ds(pl.multiple_of(o * half, LANES), half)
    my_cols = pl.ds(pl.multiple_of(o * vcols, LANES), vcols)
    other_cols = pl.ds(pl.multiple_of(other * vcols, LANES), vcols)
    kept_half = pl.ds(pl.multiple_of(outward * half, LANES), half)
    host_half = pl.ds(pl.multiple_of(inward * half, LANES), half)
    my_rows = pl.ds(pl.multiple_of(o * part, 16), part)

    local = [
        pltpu.make_async_copy(x_hbm.at[0, my_rows, :], xr, loc_sem.at[0]),
        pltpu.make_async_copy(gain_hbm, gain, loc_sem.at[1]),
        pltpu.make_async_copy(w_hbm.at[0], wbuf.at[w_at], loc_sem.at[2]),
        pltpu.make_async_copy(down_hbm.at[0], dn.at[:, :, my_half], loc_sem.at[3]),
        pltpu.make_async_copy(up_hbm.at[0], ucat.at[pl.ds(0, panels), :, my_cols], loc_sem.at[4]),
        pltpu.make_async_copy(q_hbm.at[0], qb, loc_sem.at[5]),
        pltpu.make_async_copy(k_hbm.at[0], kb.at[s], loc_sem.at[6]),
    ]
    for copy in local:
        copy.start()

    for step in range(n):
        b = step * chip_rows - min(step * chip_rows // LANES * LANES, width - win)

        @pl.when(s == step)
        def _():
            if b:
                wbuf[0:b, :] = jnp.zeros((b, vcols2), bf16)
            rest = win - b - chip_rows
            if rest:
                wbuf[win - rest : win, :] = jnp.zeros((rest, vcols2), bf16)

    for t in range(1, n):

        @pl.when(t > s)
        def _():
            kb[t] = jnp.zeros(kb.shape[1:], bf16)
            vall[t] = jnp.zeros(vall.shape[1:], bf16)

    local[0].wait()
    local[1].wait()
    rows = xr[...].astype(f32)
    inv = lax.rsqrt(jnp.mean(rows * rows, axis=1, keepdims=True) + norm_eps)
    xb[s] = (xr[...].astype(f32) * inv * gain[...]).astype(bf16)

    pl.semaphore_wait(barrier, jnp.where(end, 3, 5))

    def chunk(q, up):
        first_half = q < CHUNKS // 2
        at = (up if first_half else 1 - up) * half + (q % 2) * wide
        return pl.ds(pl.multiple_of(at, LANES), sizes[q % 2])

    def x_copy(t, q, up, sem, device):
        at = xb.at[t, :, chunk(q, up)]
        return remote(at, at, sem, x_recv.at[t, q], device)

    def x_in(which, t, q):
        return x_copy(t, q, inward, xi_send.at[which, q], peer(jnp.where(end, near_inner, far_inner)))

    def x_out(which, t, q):
        return x_copy(t, q, outward, xo_send.at[which, q], peer(near_end))

    def x_arrived(t, q, up):
        x_copy(t, q, up, xi_send.at[0, q], peer(s, other)).wait_recv()

    w_copy = remote(w_hbm.at[0], wbuf.at[w_at], ex_send.at[0], ex_recv.at[0], peer(s, other))
    dn_copy = remote(down_hbm.at[0], dn.at[:, :, my_half], ex_send.at[1], ex_recv.at[1], peer(s, other))
    up_copy = remote(
        up_hbm.at[0], ucat.at[pl.ds(0, panels), :, my_cols], ex_send.at[2], ex_recv.at[2], peer(s, other)
    )

    per_group = panels // 2
    mine = pl.ds(g * per_group, per_group)
    theirs = pl.ds((1 - g) * per_group, per_group)
    my_up = pl.ds(panels + g * per_group, per_group)
    their_up = pl.ds(panels + (1 - g) * per_group, per_group)
    ph_z = remote(down_hbm.at[0, mine], hdn.at[mine], ph_send.at[0], ph_recv.at[0], peer(near_inner))
    ph_y = remote(hdn.at[mine], hdn.at[mine], ph_send.at[1], ph_recv.at[1], peer(s, o, 1 - g))
    ph_c = [
        remote(hdn.at[mine], hdn.at[mine], ph_send.at[2], ph_recv.at[2], peer(s, other)),
        remote(hdn.at[theirs], hdn.at[theirs], ph_send.at[3], ph_recv.at[3], peer(s, other)),
    ]

    def up_ref(which, cols):
        return ucat.at[which, :, cols]

    uh_z = remote(up_hbm.at[0, mine], up_ref(my_up, my_cols), uh_send.at[0], uh_recv.at[0], peer(near_inner))
    uh_y = remote(
        up_ref(my_up, my_cols), up_ref(my_up, my_cols), uh_send.at[1], uh_recv.at[1], peer(s, o, 1 - g)
    )
    uh_y_in = remote(
        up_ref(their_up, my_cols), up_ref(their_up, my_cols), uh_send.at[1], uh_recv.at[1], peer(s, o, 1 - g)
    )
    ph_y_in = remote(hdn.at[theirs], hdn.at[theirs], ph_send.at[1], ph_recv.at[1], peer(s, o, 1 - g))
    uh_c = [
        remote(up_ref(which, my_cols), up_ref(which, my_cols), uh_send.at[2 + at], uh_recv.at[2 + at], peer(s, other))
        for at, which in enumerate((my_up, their_up))
    ]
    uh_c_in = [
        remote(up_ref(which, other_cols), up_ref(which, other_cols), uh_send.at[2 + at], uh_recv.at[2 + at], peer(s, other))
        for at, which in enumerate((my_up, their_up))
    ]

    def k_up(t):
        return remote(kb.at[t], kb.at[t], k_send.at[t], k_recv.at[t], peer(jnp.minimum(s + 1, n - 1)))

    ends, slot_of, rank_of = [], [], []
    run = jnp.int32(0)
    for r in range(requests):
        run = run + lengths[r]
        ends.append(run)
        adapter = adapters[r]
        slot_of.append(slots[adapter])
        rank_of.append(ranks[adapter])

    def request_at(position):
        found = jnp.zeros(position.shape, jnp.int32)
        for r in range(requests):
            found = found + (position >= ends[r]).astype(jnp.int32)
        return found

    def token_facts(t):
        req = request_at(t * tok + o * part + lax.broadcasted_iota(jnp.int32, (part, 1), 0))
        slot_t = jnp.zeros((part, 1), jnp.int32)
        rank_t = jnp.ones((part, 1), jnp.int32)
        for r in range(requests):
            slot_t = jnp.where(req == r, slot_of[r], slot_t)
            rank_t = jnp.where(req == r, rank_of[r], rank_t)
        return slot_t, rank_t

    def masked(low, t, chip):
        slot_t, rank_t = token_facts(t)
        column = lax.broadcasted_iota(jnp.int32, (part, low_width), 1)
        start = (slot_t - chip * panels) * rank_width
        return jnp.where((column >= start) & (column < start + rank_t), low, 0.0).astype(bf16), rank_t

    def contract(a, b):
        return lax.dot_general(a, b, (((1,), (1,)), ((), ())), preferred_element_type=f32)

    def raise_by(low, rank_t, at):
        up = ucat[pl.ds(at, panels)].reshape(low_width, vcols2)
        raised = jnp.dot(low, up, preferred_element_type=f32)
        return raised * (adapter_strength / rank_t.astype(f32))

    def base_of(t):
        return jnp.dot(xb[t, :, x_window], wbuf[...], preferred_element_type=f32)

    def inner_partial(t):
        low, rank_t = masked(contract(xb[t], dn[...].reshape(low_width, width)), t, s)
        pown[t] = base_of(t) + raise_by(low, rank_t, 0)

    def hosted_partial(t):
        low, rank_t = masked(contract(xb[t, :, host_half], hdn[...].reshape(low_width, half)), t, near_end)
        pown[t] = pown[t] + raise_by(low, rank_t, panels)

    def end_partial(t):
        panel = dn[:, :, kept_half].reshape(low_width, half)
        low, rank_t = masked(contract(xb[t, :, kept_half], panel), t, s)
        pbuf[t] = (base_of(t) + raise_by(low, rank_t, 0)).astype(bf16)

    def p_copy(t):
        return remote(pbuf.at[t], prec.at[t], p_send.at[t], p_recv.at[t], peer(near_inner))

    def s_copy(t):
        return remote(sbuf.at[t], srec.at[t], s_send.at[t], s_recv.at[t], peer(far_inner))

    def v_out(t, core):
        cols = pl.ds(pl.multiple_of(core * vcols, LANES), vcols)
        return remote(
            vbuf.at[t, :, cols], vall.at[t, o], v_send.at[t, core], v_recv.at[t, o], peer(near_end, core)
        )

    def v_core(t):
        return remote(vbuf.at[t, :, other_cols], vall.at[t, o], vc_send.at[t], v_recv.at[t, o], peer(s, other))

    def v_arrived(t, core):
        remote(vall.at[t, core], vall.at[t, core], vc_send.at[t], v_recv.at[t, core], peer(s, other)).wait_recv()

    def weights_ready():
        for at in (2, 3, 4):
            local[at].wait()
        w_copy_in = remote(w_hbm.at[0], wbuf.at[w_at], ex_send.at[0], ex_recv.at[0], peer(s, other))
        w_copy_in.wait_recv()
        up_copy.wait_recv()

    def scores_of():
        keys = kb[...].reshape(total, vcols)
        key_at = lax.broadcasted_iota(jnp.int32, (1, total), 1)
        query_at = s * tok + lax.broadcasted_iota(jnp.int32, (tok, 1), 0)
        live = (key_at <= query_at) & (key_at > query_at - WINDOW)
        live = live & (request_at(query_at) == request_at(key_at))
        for h in range(qb.shape[1] // HEAD_SIZE):
            kv = h // group
            scores = (
                contract(qb[:, h * HEAD_SIZE : (h + 1) * HEAD_SIZE], keys[:, kv * HEAD_SIZE : (kv + 1) * HEAD_SIZE])
                * query_scale
            )
            scores = jnp.where(live, scores, -1e30)
            weights = jnp.exp(scores - jnp.max(scores, axis=1, keepdims=True))
            soft = weights / jnp.sum(weights, axis=1, keepdims=True)
            prob[h] = soft.astype(bf16)

    @pl.when(end)
    def _():
        @pl.when(o == host_core)
        def _():
            ph_z.start()

        for q in range(CHUNKS):
            x_in(0, s, q).start()
        w_copy.start()
        up_copy.start()

        @pl.when(o != host_core)
        def _():
            dn_copy.start()

        uh_z.start()
        local[6].wait()

        @pl.when(s == 0)
        def _():
            k_up(s).start()

        weights_ready()

        @pl.when(o == host_core)
        def _():
            dn_kept = dn.at[:, :, kept_half]
            remote(dn_kept, dn_kept, ex_send.at[1], ex_recv.at[1], peer(s, other)).wait_recv()

        end_partial(s)
        p_copy(s).start()
        for t in (near_inner, far_inner, far_end):
            for q in range(CHUNKS // 2):
                x_arrived(t, q, outward)
            end_partial(t)
            p_copy(t).start()

        local[5].wait()

        @pl.when(s == n - 1)
        def _():
            for t in range(n - 1):
                k_up(t).wait_recv()

        scores_of()

        for t in range(n):

            @pl.when((t == 0) | (s == n - 1))
            def _():
                v_arrived(t, 0)
                v_arrived(t, 1)

    def add_end(t):
        p_copy(t).wait_recv()
        total_here = pown[t] + prec[t].astype(f32)
        pown[t] = total_here
        sbuf[t] = total_here.astype(bf16)

        @pl.when(low_side | (t < n // 2))
        def _():
            s_copy(t).start()

    def finish(t):
        s_copy(t).wait_recv()
        value = (pown[t] + srec[t].astype(f32)).astype(bf16)
        vbuf[t] = value

        @pl.when((t == 0) | (s == n - 2))
        def _():
            v_out(t, 0).start()
            v_out(t, 1).start()

        @pl.when(t <= s)
        def _():
            v_core(t).start()
            vall[t, o] = vbuf[t, :, my_cols]

    @pl.when(inner)
    def _():
        for q in range(CHUNKS):
            x_in(0, s, q).start()
            if q < CHUNKS // 2:
                x_out(0, s, q).start()
        w_copy.start()
        dn_copy.start()
        up_copy.start()
        weights_ready()
        dn_other = dn.at[:, :, pl.ds(pl.multiple_of(other * half, LANES), half)]
        remote(dn_other, dn_other, ex_send.at[1], ex_recv.at[1], peer(s, other)).wait_recv()
        inner_partial(s)
        for q in range(CHUNKS):
            x_arrived(far_inner, q, outward)
            if q < CHUNKS // 2:
                x_out(1, far_inner, q).start()
            x_arrived(near_end, q, inward)
            x_in(1, near_end, q).start()
            if q == 1:

                @pl.when(o == host_core)
                def _():
                    ph_z.wait_recv()
                    ph_y.start()
                    ph_c[0].start()

        inner_partial(near_end)
        uh_z.wait_recv()
        uh_y.start()
        uh_c[0].start()
        local[6].wait()

        @pl.when(s == 1)
        def _():
            k_up(0).wait_recv()
            k_up(0).start()

        k_up(s).start()
        x_arrived(far_end, 0, outward)
        x_out(2, far_end, 0).start()
        inner_partial(far_inner)
        x_arrived(far_end, 1, outward)
        x_out(2, far_end, 1).start()
        uh_y_in.wait_recv()
        uh_c[1].start()

        @pl.when(o == host_core)
        def _():
            ph_y_in.wait_recv()
            ph_c[1].start()

        @pl.when(o != host_core)
        def _():
            ph_c[0].wait_recv()
            ph_c[1].wait_recv()

        uh_c_in[0].wait_recv()
        uh_c_in[1].wait_recv()
        for t in (near_end, s, far_inner):
            hosted_partial(t)
            add_end(t)
        for q in range(2, CHUNKS):
            x_arrived(far_end, q, outward)
        inner_partial(far_end)
        hosted_partial(far_end)
        add_end(far_end)
        local[5].wait()

        @pl.when(s == n - 2)
        def _():
            for t in range(n - 2):
                k_up(t).wait_recv()
                k_up(t).start()

        scores_of()

        @pl.when(s == 1)
        def _():
            finish(1)
            finish(0)

        @pl.when(s == n - 2)
        def _():
            for t in range(n):
                finish(t)

        for t in range(n - 1):

            @pl.when(t <= s)
            def _():
                v_arrived(t, other)

    values = vall[...].reshape(total, vcols)
    for h in range(qb.shape[1] // HEAD_SIZE):
        kv = h // group
        ob[:, h * HEAD_SIZE : (h + 1) * HEAD_SIZE] = jnp.dot(
            prob[h], values[:, kv * HEAD_SIZE : (kv + 1) * HEAD_SIZE], preferred_element_type=f32
        ).astype(bf16)
    result = pltpu.make_async_copy(ob, out_hbm.at[0], loc_sem.at[7])
    result.start()

    w_copy.wait_send()
    up_copy.wait_send()

    @pl.when(inner | (o != host_core))
    def _():
        dn_copy.wait_send()

    for q in range(CHUNKS):
        x_in(0, s, q).wait_send()

    @pl.when(s < n - 1)
    def _():
        k_up(s).wait_send()

    @pl.when(end)
    def _():
        @pl.when(o == host_core)
        def _():
            ph_z.wait_send()

        uh_z.wait_send()
        for t in range(n):
            p_copy(t).wait_send()

    @pl.when(inner)
    def _():
        for q in range(CHUNKS):
            x_in(1, near_end, q).wait_send()
        for which in range(3):
            for q in range(CHUNKS // 2):
                x_out(which, s, q).wait_send()

        @pl.when(o == host_core)
        def _():
            ph_y.wait_send()
            ph_c[0].wait_send()
            ph_c[1].wait_send()

        uh_y.wait_send()
        uh_c[0].wait_send()
        uh_c[1].wait_send()
        for t in range(n):

            @pl.when(t < s)
            def _():
                k_up(t).wait_send()

            @pl.when(low_side | (t < n // 2))
            def _():
                s_copy(t).wait_send()

            @pl.when((t == 0) | (s == n - 2))
            def _():
                v_out(t, 0).wait_send()
                v_out(t, 1).wait_send()

            @pl.when(t <= s)
            def _():
                v_core(t).wait_send()

    result.wait()


def fused(
    n,
    layer_input_rows,
    encoded_query_rows,
    encoded_key_rows,
    layer_norm_gain,
    base_value_matrix,
    adapter_down_panels,
    adapter_up_panels,
    request_token_lengths,
    adapter_per_request,
    rank_per_adapter,
    slot_per_adapter,
):
    f32, bf16 = jnp.float32, jnp.bfloat16
    tok, width = layer_input_rows.shape[1:]
    part, half = tok // 2, width // 2
    panels, _, rank_width = adapter_down_panels.shape[1:]
    vcols = adapter_up_panels.shape[3]
    qcols = encoded_query_rows.shape[2]
    chip_rows = width // n
    pads = [i * chip_rows % LANES for i in range(n)]
    win = -(-(max(pads) + chip_rows) // LANES) * LANES
    total = n * tok
    dma = pltpu.SemaphoreType.DMA
    any_spec = pl.BlockSpec(memory_space=pl.ANY)
    smem = pl.BlockSpec(memory_space=pltpu.SMEM)
    return pl.pallas_call(
        functools.partial(kernel, n),
        out_shape=jax.ShapeDtypeStruct(encoded_query_rows.shape, bf16),
        in_specs=[smem] * 4 + [any_spec] * 7,
        out_specs=any_spec,
        scratch_shapes=[
            pltpu.VMEM((part, width), bf16),
            pltpu.VMEM((1, width), f32),
            pltpu.VMEM((n, part, width), bf16),
            pltpu.VMEM((win, 2 * vcols), bf16),
            pltpu.VMEM((panels, rank_width, width), bf16),
            pltpu.VMEM((panels, rank_width, half), bf16),
            pltpu.VMEM((2 * panels, rank_width, 2 * vcols), bf16),
            pltpu.VMEM((tok, qcols), bf16),
            pltpu.VMEM((n, tok, vcols), bf16),
            pltpu.VMEM((n, part, 2 * vcols), f32),
            pltpu.VMEM((n, part, 2 * vcols), bf16),
            pltpu.VMEM((n, part, 2 * vcols), bf16),
            pltpu.VMEM((n, part, 2 * vcols), bf16),
            pltpu.VMEM((n, part, 2 * vcols), bf16),
            pltpu.VMEM((n, part, 2 * vcols), bf16),
            pltpu.VMEM((n, 2, part, vcols), bf16),
            pltpu.VMEM((qcols // HEAD_SIZE, tok, total), bf16),
            pltpu.VMEM((tok, qcols), bf16),
            dma((8,)),
            dma((2, CHUNKS)),
            dma((3, CHUNKS // 2)),
            dma((n, CHUNKS)),
            dma((3,)),
            dma((3,)),
            dma((4,)),
            dma((4,)),
            dma((4,)),
            dma((4,)),
            dma((n,)),
            dma((n,)),
            dma((n,)),
            dma((n,)),
            dma((n,)),
            dma((n,)),
            dma((n, 2)),
            dma((n,)),
            dma((n, 2)),
        ],
        compiler_params=pltpu.CompilerParams(
            collective_id=0, has_side_effects=True, vmem_limit_bytes=56 * 1024 * 1024
        ),
    )(
        request_token_lengths,
        adapter_per_request,
        rank_per_adapter,
        slot_per_adapter,
        layer_input_rows,
        encoded_query_rows,
        encoded_key_rows,
        layer_norm_gain,
        base_value_matrix,
        jnp.swapaxes(adapter_down_panels, 2, 3),
        adapter_up_panels,
    )


def solution(mesh):
    in_specs = (
        P("segment", ("groups", "seq"), None),
        P("segment", ("groups", "seq"), "owner"),
        P("segment", ("groups", "seq"), "owner"),
        P("segment", None),
        P("segment", ("seq", "owner"), None),
        P("segment", "seq", "owner", None),
        P("segment", "seq", None, "owner"),
        P("groups"),
        P("groups"),
        P(),
        P(),
    )
    out_specs = P("segment", ("groups", "seq"), "owner")
    n = mesh.shape["seq"]
    small = mesh.shape["owner"] == 2 and mesh.shape["groups"] == 2 and n == 4
    return jax.shard_map(
        functools.partial(fused, n) if small else per_device, mesh=mesh, in_specs=in_specs, out_specs=out_specs, check_vma=False
    )
```

time: 47.3 us -> 42.4 us (0.90)
  the two profiles are of different devices: /device:TPU:0 before, /device:TPU:25 now
where the time goes in v1:
time: 42.4 us; the launch traced here: 42.3 us
  Pallas kernels  40.7 us (96%)
  local copies, waits for them, and re-layouts  1.57 us (4%)
    pallas_call x1, Pallas kernels, fused(): pl.pallas_call(functools.partial(kernel, n), out_shape=jax.ShapeDtypeStru...  40.7 us
    unnamed x1, local copies, waits for them, and re-layouts  1.57 us

profile of v1, /device:TPU:25, one launch (start us, length us, event | category | flops | bytes accessed | tf_op | source)
XLA Modules:
  0.0 42.3 jit_solution(213360069431167563)
XLA Ops:
  0.0 40.7 %shard_map.109 = bf16[1,64,1024]{2,1,0:T(8,128)(2,1)} custom-call(s32[4]{0:T(128)} %lengths.1, s32[4]{0:T(128)} %adapters.1, s32[8]{0:T(128)} %ranks.1, s32[8]{0:T(128)} %slots.1, bf16[1,64,5376]{2,1,0:T(8,128)(2,1)} %x_hbm.1, bf16[1,64,1024]{2,1,0:T(8,128)(2,1)} %q_hbm.1, bf16[1,64,512]{2,1,0:T(8,128)(2,1)} %k_hbm.1, f32[1,5376]{1,0:T(1,128)} %gain_hbm.1, ...), custom_call_target="tpu_custom_call" | custom-call | tf_op jit(solution)/shard_map/pallas_call | solution.py:758
  40.7 1.6 %copy.13 = bf16[1,64,1024]{2,1,0:T(8,128)(2,1)} copy(bf16[1,64,1024]{2,1,0:T(8,128)(2,1)} %shard_map.109) | data formatting | bytes 262144

commit v2 on v1

v2 whole, which is shorter than its diff:
```python
import functools

import jax
import jax.numpy as jnp
from jax import lax
from jax.experimental import pallas as pl
from jax.experimental.pallas import tpu as pltpu
from jax.sharding import PartitionSpec as P

WINDOW = 1024
HEADS = 16
KEY_VALUE_HEADS = 8
HEAD_SIZE = 128


query_scale = 168.0 ** (-0.5)
adapter_strength = 32.0
norm_eps = 1e-06


def broadcast(x, axis, root):
    mine = lax.axis_index(axis) == root
    return lax.psum(jnp.where(mine, x, jnp.zeros_like(x)), axis)


def from_behind(value, axis, steps):
    count = lax.axis_size(axis)
    first, last = (max(0, -steps), min(count, count - steps))
    return lax.ppermute(value, axis, [(source, source + steps) for source in range(first, last)])


def per_device(
    layer_input_rows,
    encoded_query_rows,
    encoded_key_rows,
    layer_norm_gain,
    base_value_matrix,
    adapter_down_panels,
    adapter_up_panels,
    request_token_lengths,
    adapter_per_request,
    rank_per_adapter,
    slot_per_adapter,
):
    hidden = layer_input_rows[0]
    row_count = hidden.shape[0]
    seq_now = lax.axis_index("seq")
    owner_now = lax.axis_index("owner")
    reach_count = min(WINDOW // row_count, lax.axis_size("seq") - 1)
    requests = request_token_lengths.shape[0]
    library = slot_per_adapter.shape[0]
    slots_here = adapter_down_panels.shape[1]
    rows_halved = adapter_down_panels.shape[2]
    rank_span_width = adapter_down_panels.shape[3]
    key_value_halved = adapter_up_panels.shape[3]
    group_size = HEADS // KEY_VALUE_HEADS
    request_ends = jnp.cumsum(request_token_lengths)
    position = seq_now * row_count + jnp.arange(row_count, dtype=jnp.int32)
    context = seq_now * row_count + jnp.arange(-reach_count * row_count, row_count, dtype=jnp.int32)
    request_lookup = jnp.sum((position[:, None] >= request_ends[None, :]).astype(jnp.int32), axis=1)
    request_ctx = jnp.sum((context[:, None] >= request_ends[None, :]).astype(jnp.int32), axis=1)
    live_mask = (context[None, :] <= position[:, None]) & (
        context[None, :] > position[:, None] - WINDOW
    )
    live_mask = (
        live_mask & (context[None, :] >= 0) & (request_ctx[None, :] == request_lookup[:, None])
    )
    choose = adapter_per_request[:, None] == jnp.arange(library, dtype=jnp.int32)[None, :]
    slot_of = jnp.sum(jnp.where(choose, slot_per_adapter[None, :], 0), axis=1)
    rank_lookup = jnp.sum(jnp.where(choose, rank_per_adapter[None, :], 0), axis=1)
    scale_lookup = adapter_strength / rank_lookup.astype(jnp.float32)
    in_request = request_lookup[:, None] == jnp.arange(requests, dtype=jnp.int32)[None, :]
    column_live = jnp.arange(rank_span_width, dtype=jnp.int32)[None, :] < rank_lookup[:, None]
    row_gain_weight = jnp.where(in_request, scale_lookup[None, :], jnp.float32(0.0))
    down_panel_here = adapter_down_panels[0]
    up_panel_here = adapter_up_panels[0]
    queries = encoded_query_rows[0]
    keys_own = encoded_key_rows[0]
    key_heads = keys_own.shape[1] // HEAD_SIZE
    wide_rows = hidden.astype(jnp.float32)
    normalized_rows = wide_rows * lax.rsqrt(
        jnp.mean(wide_rows * wide_rows, axis=1, keepdims=True) + norm_eps
    )
    normalized_rows = (normalized_rows * layer_norm_gain[0][None, :]).astype(jnp.bfloat16)
    normed_half = lax.dynamic_slice_in_dim(normalized_rows, owner_now * rows_halved, rows_halved, 1)
    full_value = jnp.dot(
        normalized_rows,
        lax.all_gather(base_value_matrix[0], ("seq", "owner"), axis=0, tiled=True),
        preferred_element_type=jnp.float32,
    )
    value_base_rows = lax.dynamic_slice_in_dim(
        full_value, owner_now * key_value_halved, key_value_halved, 1
    )

    def fetch_one(reduced_rows, request_index):
        owner_slot = slot_of[request_index]
        holder = owner_slot // slots_here
        local_slot = owner_slot % slots_here
        down_local = lax.dynamic_slice_in_dim(down_panel_here, local_slot, 1, 0)
        up_local = lax.dynamic_slice_in_dim(up_panel_here, local_slot, 1, 0)
        down_piece, up_piece = (
            broadcast(down_local, "seq", holder),
            broadcast(up_local, "seq", holder),
        )
        keep_mask = in_request[:, request_index][:, None] & column_live[request_index][None, :]
        matrix_product = jnp.dot(normed_half, down_piece[0], preferred_element_type=jnp.float32)
        return (reduced_rows + jnp.where(keep_mask, matrix_product, jnp.float32(0.0)), up_piece[0])

    start_low = jnp.zeros((row_count, rank_span_width), jnp.float32)
    reduced_rows, panels_up = lax.scan(fetch_one, start_low, jnp.arange(requests, dtype=jnp.int32))
    reduced_rows = lax.psum(reduced_rows, "owner").astype(jnp.bfloat16)
    raised_rows = jnp.einsum(
        "tr,qrk->qtk", reduced_rows, panels_up, preferred_element_type=jnp.float32
    )
    adapter_value = jnp.sum(row_gain_weight.T[:, :, None] * raised_rows, axis=0)
    value_output_rows = (value_base_rows + adapter_value).astype(jnp.bfloat16)
    key_parts = []
    value_parts = []
    for shift_by in range(reach_count, 0, -1):
        key_piece, value_piece = from_behind((keys_own, value_output_rows), "seq", shift_by)
        key_parts.append(key_piece)
        value_parts.append(value_piece)
    keys_all = jnp.concatenate(key_parts + [keys_own], axis=0)
    values_all = jnp.concatenate(value_parts + [value_output_rows], axis=0)
    query_view = queries.reshape(row_count, key_heads, group_size, HEAD_SIZE)
    key_view = keys_all.reshape(-1, key_heads, HEAD_SIZE)
    value_view = values_all.reshape(-1, key_heads, HEAD_SIZE)
    head_outputs = []
    for head_index in range(key_heads):
        query_head = query_view[:, head_index]
        scores = (
            jnp.einsum(
                "tcd,jd->ctj",
                query_head,
                key_view[:, head_index],
                preferred_element_type=jnp.float32,
            )
            * query_scale
        )
        scores = jnp.where(live_mask[None], scores, jnp.float32(-1e30))
        row_max = jnp.max(scores, axis=-1, keepdims=True)
        weights = jnp.exp(scores - row_max)
        row_total = jnp.sum(weights, axis=-1, keepdims=True)
        softmax_rows = (weights / row_total).astype(jnp.bfloat16)
        mixed = jnp.einsum(
            "ctj,jd->tcd",
            softmax_rows,
            value_view[:, head_index],
            preferred_element_type=jnp.float32,
        )
        head_outputs.append(mixed.astype(jnp.bfloat16).reshape(row_count, group_size * HEAD_SIZE))
    result = jnp.concatenate(head_outputs, axis=1)
    return result[None]


LANES = 128
CHUNKS = 4


def kernel(
    n,
    x_hbm,
    q_hbm,
    k_hbm,
    gain_hbm,
    w_hbm,
    down_hbm,
    up_hbm,
    lengths_hbm,
    adapters_hbm,
    ranks_hbm,
    slots_hbm,
    out_hbm,
    lengths,
    adapters,
    ranks,
    slots,
    xr,
    gain,
    xb,
    wbuf,
    dn,
    hdn,
    dnt,
    ucat,
    qb,
    kb,
    pown,
    pbuf,
    prec,
    sbuf,
    srec,
    vbuf,
    vall,
    prob,
    ob,
    loc_sem,
    x_send,
    x_recv,
    ex_send,
    ex_recv,
    ph_send,
    ph_recv,
    uh_send,
    uh_recv,
    k_send,
    k_recv,
    p_send,
    p_recv,
    s_send,
    s_recv,
    v_send,
    v_recv,
):
    f32, bf16 = jnp.float32, jnp.bfloat16
    s = lax.axis_index("seq")
    o = lax.axis_index("owner")
    g = lax.axis_index("groups")
    other = 1 - o
    tok, width = x_hbm.shape[1], x_hbm.shape[2]
    part = tok // 2
    half = width // 2
    win, vcols2 = wbuf.shape
    vcols = vcols2 // 2
    slab = w_hbm.shape[1]
    panels, rank_width = dn.shape[0], dn.shape[1]
    low_width = panels * rank_width
    rank_part = rank_width // 2
    chip_rows = width // n
    requests = lengths.shape[0]
    total = n * tok
    group = HEADS // KEY_VALUE_HEADS
    q_heads = qb.shape[1] // HEAD_SIZE
    wide = -(-half // (2 * LANES)) * LANES
    sizes = (wide, half - wide)

    def peer(seq, owner=None, groups=None):
        return {
            "seq": seq,
            "owner": o if owner is None else owner,
            "groups": g if groups is None else groups,
        }

    def remote(src, dst, send, recv, device):
        return pltpu.make_async_remote_copy(
            src_ref=src,
            dst_ref=dst,
            send_sem=send,
            recv_sem=recv,
            device_id=device,
            device_id_type=pl.DeviceIdType.MESH,
        )

    def arrived(ref, sem):
        remote(ref, ref, sem, sem, peer(s, other)).wait_recv()

    def sent(ref, sem):
        remote(ref, ref, sem, sem, peer(s, other)).wait_send()

    barrier = pltpu.get_barrier_semaphore()

    def greet(device):
        pl.semaphore_signal(barrier, inc=1, device_id=device, device_id_type=pl.DeviceIdType.MESH)

    my_rows = pl.ds(pl.multiple_of(o * part, 16), part)
    my_half = pl.ds(pl.multiple_of(o * half, LANES), half)
    other_half = pl.ds(pl.multiple_of(other * half, LANES), half)
    my_cols = pl.ds(pl.multiple_of(o * vcols, LANES), vcols)
    other_cols = pl.ds(pl.multiple_of(other * vcols, LANES), vcols)

    def half_at(which):
        return pl.ds(which * half, half)

    ends, slot_of, rank_of = [], [], []

    def read_tables():
        for at in range(7, 11):
            local[at].wait()
        run = jnp.int32(0)
        for r in range(requests):
            run = run + lengths[r]
            ends.append(run)
            adapter = adapters[r]
            slot_of.append(slots[adapter])
            rank_of.append(ranks[adapter])

    def request_at(position):
        found = jnp.zeros(position.shape, jnp.int32)
        for r in range(requests):
            found = found + (position >= ends[r]).astype(jnp.int32)
        return found

    def token_facts(first, count):
        row = lax.broadcasted_iota(jnp.int32, (count * part, 1), 0)
        position = (first + row // part) * tok + o * part + row % part
        req = request_at(position)
        slot_t = jnp.zeros(row.shape, jnp.int32)
        rank_t = jnp.ones(row.shape, jnp.int32)
        for r in range(requests):
            slot_t = jnp.where(req == r, slot_of[r], slot_t)
            rank_t = jnp.where(req == r, rank_of[r], rank_t)
        return slot_t, rank_t

    def masked(low, slot_t, rank_t, chip):
        column = lax.broadcasted_iota(jnp.int32, low.shape, 1)
        start = (slot_t - chip * panels) * rank_width
        return jnp.where((column >= start) & (column < start + rank_t), low, 0.0).astype(bf16)

    def dot(a, b):
        return jnp.dot(a, b, preferred_element_type=f32)

    def window_of(c):
        at = min(c * chip_rows // LANES * LANES, width - win)
        return at, c * chip_rows - at

    def rows_of(first, count, columns):
        return xb[first : first + count, :, columns].reshape(count * part, columns.size)

    def partial(c, first, count, own, hosted, chip):
        slot_t, rank_t = token_facts(first, count)
        at, _ = window_of(c)
        base = dot(rows_of(first, count, pl.ds(at, win)), wbuf[...])
        if hosted is None:
            low = dot(rows_of(first, count, half_at(own)), dnt[half_at(own), :low_width])
            low = masked(low, slot_t, rank_t, c)
            raised = dot(low, ucat[:panels].reshape(low_width, vcols2))
        else:
            both = dot(rows_of(first, count, half_at(hosted)), dnt[half_at(hosted), :])
            low = both[:, :low_width] + dot(rows_of(first, count, half_at(own)), dnt[half_at(own), :low_width])
            low = jnp.concatenate(
                [masked(low, slot_t, rank_t, c), masked(both[:, low_width:], slot_t, rank_t, chip)], axis=1
            )
            raised = dot(low, ucat[...].reshape(2 * low_width, vcols2))
        value = base + raised * (adapter_strength / rank_t.astype(f32))
        return value.reshape(count, part, vcols2)

    def chunk(q, up):
        at = (up if q < CHUNKS // 2 else 1 - up) * half + (q % 2) * wide
        return pl.ds(at, sizes[q % 2])

    local = [
        pltpu.make_async_copy(x_hbm.at[0, my_rows, :], xr, loc_sem.at[0]),
        pltpu.make_async_copy(gain_hbm, gain, loc_sem.at[1]),
        pltpu.make_async_copy(w_hbm.at[0], wbuf.at[pl.ds(0, slab)], loc_sem.at[2]),
        pltpu.make_async_copy(down_hbm.at[0], dn.at[:, :, my_half], loc_sem.at[3]),
        pltpu.make_async_copy(up_hbm.at[0], ucat.at[pl.ds(0, panels), :, my_cols], loc_sem.at[4]),
        pltpu.make_async_copy(q_hbm.at[0], qb, loc_sem.at[5]),
        pltpu.make_async_copy(k_hbm.at[0], kb.at[s], loc_sem.at[6]),
        pltpu.make_async_copy(lengths_hbm, lengths, loc_sem.at[7]),
        pltpu.make_async_copy(adapters_hbm, adapters, loc_sem.at[8]),
        pltpu.make_async_copy(ranks_hbm, ranks, loc_sem.at[9]),
        pltpu.make_async_copy(slots_hbm, slots, loc_sem.at[10]),
    ]

    def slab_at(c):
        _, pad = window_of(c)
        return pl.ds(pl.multiple_of(pad + o * slab, 16), slab)

    def transpose_panels(source, which, at):
        for piece in range(0, half, half // 3):
            rows = source[:, :, pl.ds(which * half + piece if source.shape[2] == width else piece, half // 3)]
            dnt[pl.ds(which * half + piece, half // 3), at : at + low_width] = rows.reshape(
                low_width, half // 3
            ).T

    def opening(c, greetings, count):
        local[0].start()
        local[1].start()
        w_local = pltpu.make_async_copy(w_hbm.at[0], wbuf.at[slab_at(c)], loc_sem.at[2])
        w_local.start()
        for at in range(3, 11):
            local[at].start()
        for device in greetings:
            greet(device)
        _, pad = window_of(c)
        if pad:
            wbuf[0:pad, :] = jnp.zeros((pad, vcols2), bf16)
        rest = win - pad - chip_rows
        if rest:
            wbuf[win - rest : win, :] = jnp.zeros((rest, vcols2), bf16)
        for t in range(c + 1, n):
            kb[t] = jnp.zeros(kb.shape[1:], bf16)
            vall[t] = jnp.zeros(vall.shape[1:], bf16)
        local[0].wait()
        local[1].wait()
        rows = xr[...].astype(f32)
        inv = lax.rsqrt(jnp.mean(rows * rows, axis=1, keepdims=True) + norm_eps)
        xb[c] = (xr[...].astype(f32) * inv * gain[...]).astype(bf16)
        pl.semaphore_wait(barrier, count)

    def exchange(c, kept):
        w_copy = remote(w_hbm.at[0], wbuf.at[slab_at(c)], ex_send.at[0], ex_recv.at[0], peer(c, other))
        dn_copy = remote(down_hbm.at[0], dn.at[:, :, my_half], ex_send.at[1], ex_recv.at[1], peer(c, other))
        up_copy = remote(
            up_hbm.at[0], ucat.at[pl.ds(0, panels), :, my_cols], ex_send.at[2], ex_recv.at[2], peer(c, other)
        )
        return w_copy, dn_copy, up_copy

    def attend(c):
        keys = kb[...].reshape(total, vcols)
        key_at = lax.broadcasted_iota(jnp.int32, (1, total), 1)
        query_at = c * tok + lax.broadcasted_iota(jnp.int32, (tok, 1), 0)
        live = (key_at <= query_at) & (key_at > query_at - WINDOW)
        live = live & (request_at(query_at) == request_at(key_at))
        for h in range(q_heads):
            kv = h // group
            scores = (
                lax.dot_general(
                    qb[:, h * HEAD_SIZE : (h + 1) * HEAD_SIZE],
                    keys[:, kv * HEAD_SIZE : (kv + 1) * HEAD_SIZE],
                    (((1,), (1,)), ((), ())),
                    preferred_element_type=f32,
                )
                * query_scale
            )
            scores = jnp.where(live, scores, -1e30)
            weights = jnp.exp(scores - jnp.max(scores, axis=1, keepdims=True))
            soft = weights / jnp.sum(weights, axis=1, keepdims=True)
            prob[h] = soft.astype(bf16)

    result = pltpu.make_async_copy(ob, out_hbm.at[0], loc_sem.at[0])

    def mix(c):
        values = vall[...].reshape(total, vcols)
        for h in range(q_heads):
            kv = h // group
            ob[:, h * HEAD_SIZE : (h + 1) * HEAD_SIZE] = dot(
                prob[h], values[:, kv * HEAD_SIZE : (kv + 1) * HEAD_SIZE]
            ).astype(bf16)
        result.start()

    per_group = panels // 2
    mine = pl.ds(g * per_group, per_group)
    theirs = pl.ds((1 - g) * per_group, per_group)
    my_up = pl.ds(panels + g * per_group, per_group)
    their_up = pl.ds(panels + (1 - g) * per_group, per_group)
    my_piece = pl.ds(pl.multiple_of(o * rank_part, 16), rank_part)
    other_piece = pl.ds(pl.multiple_of(other * rank_part, 16), rank_part)

    def x_end(c, t, q, up, to):
        at = xb.at[t, :, chunk(q, up)]
        return remote(at, at, x_send.at[0], x_recv.at[q], peer(to))

    def x_across(t, q, up, to, forwarded):
        at = xb.at[t, :, chunk(q, up)]
        index = (7 if forwarded else 4) + min(q, 2)
        return remote(at, at, x_send.at[0], x_recv.at[index], peer(to))

    def x_outward(t, q, up, to, index):
        at = xb.at[t, :, chunk(q, up)]
        return remote(at, at, x_send.at[1], x_recv.at[index], peer(to))

    def k_up(c, t):
        return remote(kb.at[t], kb.at[t], k_send, k_recv, peer(c + 1))

    def end_program(c):
        low = c < n // 2
        i, j, f = (1, 2, 3) if low else (2, 1, 0)
        inward = int(low)
        kept = 1 - inward
        host_core = inward
        opening(c, [peer(c, other), peer(i), peer(i, other)], 3)
        w_copy, dn_copy, up_copy = exchange(c, kept)
        piece_in = remote(
            down_hbm.at[0, mine, other_piece, :], hdn.at[mine, other_piece, :], ph_send.at[1], ph_recv.at[1], peer(c, other)
        )
        piece_z = remote(
            down_hbm.at[0, mine, my_piece, :], hdn.at[mine, my_piece, :], ph_send.at[0], ph_recv.at[0], peer(i)
        )
        piece_on = remote(
            hdn.at[mine, my_piece, :], hdn.at[mine, my_piece, :], ph_send.at[0], ph_recv.at[0], peer(i)
        )
        up_z = remote(up_hbm.at[0, mine], ucat.at[my_up, :, my_cols], uh_send.at[0], uh_recv.at[0], peer(i))

        @pl.when(o == host_core)
        def _():
            piece_in.start()
            piece_z.start()
            up_z.start()
            x_end(c, c, 0, inward, i).start()

        @pl.when(o != host_core)
        def _():
            up_z.start()
            x_end(c, c, 0, inward, i).start()
            dn_copy.start()

        w_copy.start()
        up_copy.start()

        @pl.when(o != host_core)
        def _():
            arrived(hdn.at[mine, my_piece, :], ph_recv.at[1])
            piece_on.start()

        for q in range(1, CHUNKS):
            x_end(c, c, q, inward, i).start()
        if c == 0:
            local[6].wait()
            k_up(c, c).start()
        for at in (2, 3, 4):
            local[at].wait()
        read_tables()

        @pl.when(o == host_core)
        def _():
            arrived(dn.at[:, :, other_half], ex_recv.at[1])

        transpose_panels(dn, kept, 0)
        arrived(ucat.at[pl.ds(0, panels), :, other_cols], ex_recv.at[2])
        arrived(wbuf.at[pl.ds(0, slab)], ex_recv.at[0])

        def p_copy(t):
            index = 1 if t == f else 2 if t == i and not low else 0
            return remote(pbuf.at[t], prec.at[t], p_send, p_recv.at[index], peer(i))

        p_core = remote(
            pbuf.at[c, :, other_cols], prec.at[c, :, pl.ds(0, vcols)], s_send, s_recv.at[0], peer(c, other)
        )

        def end_partial(t):
            pbuf[t] = partial(c, t, 1, kept, None, c)[0].astype(bf16)

        end_partial(c)
        if low:
            p_copy(c).start()
        else:
            p_core.start()
        for index, t in enumerate((i, j, f)):
            arrived(xb.at[t, :, half_at(kept)], x_recv.at[index])
            end_partial(t)
            if low or t != i:
                p_copy(t).start()
            if not low and t == f:
                p_copy(i).start()
        local[5].wait()
        if low:
            attend(c)
            arrived(vall.at[0], v_recv.at[0])
        else:
            local[6].wait()
            arrived(kb.at[pl.ds(0, n - 1)], k_recv)
            attend(c)
            arrived(prec.at[c, :, pl.ds(0, vcols)], s_recv.at[0])
            for t in range(n):
                arrived(vall.at[t], v_recv.at[t])
            vall[c, o] = (vall[c, o].astype(f32) + pbuf[c, :, my_cols].astype(f32)).astype(bf16)
            vall[c, other] = (vall[c, other].astype(f32) + prec[c, :, 0:vcols].astype(f32)).astype(bf16)
        mix(c)

        sent(wbuf.at[pl.ds(0, slab)], ex_send.at[0])
        sent(ucat.at[pl.ds(0, panels), :, other_cols], ex_send.at[2])
        sent(hdn.at[mine, my_piece, :], ph_send.at[0])

        @pl.when(o == host_core)
        def _():
            sent(hdn.at[mine, my_piece, :], ph_send.at[1])

        @pl.when(o != host_core)
        def _():
            sent(dn.at[:, :, my_half], ex_send.at[1])

        sent(ucat.at[my_up, :, my_cols], uh_send.at[0])
        sent(xb.at[0], x_send.at[0])
        if c == 0:
            sent(kb.at[0], k_send)
            sent(pbuf, p_send)
        else:
            sent(pbuf.at[pl.ds(0, n - 1)], p_send)
            sent(pbuf.at[c, :, other_cols], s_send)
        result.wait()

    def inner_program(c):
        low = c < n // 2
        e, j, f = (0, 2, 3) if low else (3, 1, 0)
        inward = int(low)
        outward = 1 - inward
        first = min(c, e, j)
        opening(c, [peer(c, other), peer(e), peer(e, other), peer(j), peer(c, o, 1 - g)], 5)
        w_copy, dn_copy, up_copy = exchange(c, None)
        for q in range(CHUNKS):
            x_across(c, q, inward, j, False).start()
            if q < CHUNKS // 2:
                x_outward(c, q, outward, e, 0).start()
        w_copy.start()
        dn_copy.start()
        up_copy.start()
        local[6].wait()
        if not low:
            k_up(c, c).start()
        for at in (2, 3, 4):
            local[at].wait()
        read_tables()
        arrived(dn.at[:, :, other_half], ex_recv.at[1])
        transpose_panels(dn, outward, 0)
        transpose_panels(dn, inward, 0)

        def next_e(q):
            arrived(xb.at[e, :, chunk(q, inward)], x_recv.at[q])
            x_across(e, q, inward, j, True).start()

        def next_j(q):
            arrived(xb.at[j, :, chunk(q, outward)], x_recv.at[4 + q])
            x_outward(j, q, outward, e, 1).start()

        def next_f(q):
            arrived(xb.at[f, :, chunk(q, outward)], x_recv.at[7 + q])
            x_outward(f, q, outward, e, 2).start()

        def piece(which, ranks_at):
            return hdn.at[which, ranks_at, :]

        def pass_on(which, ranks_at, sem, recv, device):
            return remote(piece(which, ranks_at), piece(which, ranks_at), ph_send.at[sem], ph_recv.at[recv], device)

        def pass_up(which, sem, recv, device):
            at = ucat.at[which, :, my_cols]
            return remote(at, at, uh_send.at[sem], uh_recv.at[recv], device)

        def host_z():
            arrived(piece(mine, my_piece), ph_recv.at[0])
            pass_on(mine, my_piece, 0, 1, peer(c, o, 1 - g)).start()
            pass_on(mine, my_piece, 1, 2, peer(c, other)).start()
            arrived(ucat.at[my_up, :, my_cols], uh_recv.at[0])
            pass_up(my_up, 0, 1, peer(c, o, 1 - g)).start()
            pass_up(my_up, 1, 2, peer(c, other)).start()

        def host_y():
            arrived(piece(theirs, my_piece), ph_recv.at[1])
            pass_on(theirs, my_piece, 1, 3, peer(c, other)).start()
            arrived(ucat.at[their_up, :, my_cols], uh_recv.at[1])
            pass_up(their_up, 1, 3, peer(c, other)).start()

        def host_done():
            arrived(piece(mine, other_piece), ph_recv.at[2])
            arrived(piece(theirs, other_piece), ph_recv.at[3])
            transpose_panels(hdn, inward, low_width)
            arrived(ucat.at[my_up, :, other_cols], uh_recv.at[2])
            arrived(ucat.at[their_up, :, other_cols], uh_recv.at[3])

        if low:
            host_z()
            next_j(0)
            next_e(0)
            next_j(1)
            next_e(1)
            host_y()
            next_e(2)
            next_e(3)
            k_up(c, c).start()
            arrived(kb.at[0], k_recv)
            k_up(c, 0).start()
            host_done()
            next_f(0)
        else:
            next_j(0)
            next_j(1)
            host_z()
            next_e(0)
            next_f(0)
            next_e(1)
            host_y()
            next_f(1)
            next_e(2)
            host_done()
            next_e(3)
        arrived(ucat.at[pl.ds(0, panels), :, other_cols], ex_recv.at[2])
        arrived(wbuf.at[pl.ds(0, slab)], ex_recv.at[0])
        arrived(xb.at[j, :, half_at(inward)], x_recv.at[6])
        pown[first : first + 3] = partial(c, first, 3, outward, inward, e)
        if low:
            next_f(1)

        def s_copy(t):
            return remote(sbuf.at[t], srec.at[t], s_send, s_recv.at[t], peer(j))

        def add_end(t):
            if low or t != e:
                value = pown[t] + prec[t].astype(f32)
                pown[t] = value
                if low or t < n // 2:
                    sbuf[t] = value.astype(bf16)
                    s_copy(t).start()

        if low:
            arrived(prec.at[pl.ds(0, 3)], p_recv.at[0])
            for t in range(3):
                add_end(t)
        arrived(xb.at[f, :, half_at(inward)], x_recv.at[9])
        pown[f] = partial(c, f, 1, outward, inward, e)[0]
        if not low:
            arrived(prec.at[j], p_recv.at[0])
            add_end(j)
        arrived(prec.at[f], p_recv.at[1])
        add_end(f)
        local[5].wait()
        if not low:
            arrived(kb.at[pl.ds(0, 2)], k_recv)
            for t in range(2):
                k_up(c, t).start()
        attend(c)

        def v_end(t, core):
            cols = pl.ds(core * vcols, vcols)
            return remote(vbuf.at[t, :, cols], vall.at[t, o], v_send.at[0], v_recv.at[t], peer(e, core))

        def v_core(t):
            return remote(vbuf.at[t, :, other_cols], vall.at[t, o], v_send.at[1], v_recv.at[t], peer(c, other))

        def finish(t):
            arrived(srec.at[t], s_recv.at[t])
            vbuf[t] = (pown[t] + srec[t].astype(f32)).astype(bf16)
            if t == 0 or not low:
                v_end(t, 0).start()
                v_end(t, 1).start()
            if t <= c:
                v_core(t).start()
                vall[t, o] = vbuf[t, :, my_cols]

        if low:
            finish(1)
            finish(0)
        else:
            arrived(prec.at[c], p_recv.at[2])
            pown[c] = pown[c] + prec[c].astype(f32)
            for t in range(n):
                finish(t)
        for t in range(c + 1):
            arrived(vall.at[t, other], v_recv.at[t])
        mix(c)

        sent(wbuf.at[pl.ds(0, slab)], ex_send.at[0])
        sent(dn.at[:, :, my_half], ex_send.at[1])
        sent(ucat.at[pl.ds(0, panels), :, other_cols], ex_send.at[2])
        sent(xb.at[pl.ds(0, 2)], x_send.at[0])
        sent(xb.at[pl.ds(0, 3), :, half_at(0)], x_send.at[1])
        sent(piece(mine, my_piece), ph_send.at[0])
        sent(hdn.at[:, my_piece, :], ph_send.at[1])
        sent(ucat.at[my_up, :, my_cols], uh_send.at[0])
        sent(ucat.at[pl.ds(panels, panels), :, my_cols], uh_send.at[1])
        sent(kb.at[pl.ds(0, c + 1)], k_send)
        if low:
            sent(sbuf, s_send)
            sent(vbuf.at[0], v_send.at[0])
        else:
            sent(sbuf.at[pl.ds(0, 2)], s_send)
            sent(vbuf, v_send.at[0])
        sent(vbuf.at[pl.ds(0, c + 1), :, pl.ds(0, vcols)], v_send.at[1])
        result.wait()

    for c in range(n):

        @pl.when(s == c)
        def _():
            ends.clear()
            slot_of.clear()
            rank_of.clear()
            if c in (0, n - 1):
                end_program(c)
            else:
                inner_program(c)


def fused(
    n,
    layer_input_rows,
    encoded_query_rows,
    encoded_key_rows,
    layer_norm_gain,
    base_value_matrix,
    adapter_down_panels,
    adapter_up_panels,
    request_token_lengths,
    adapter_per_request,
    rank_per_adapter,
    slot_per_adapter,
):
    f32, bf16 = jnp.float32, jnp.bfloat16
    tok, width = layer_input_rows.shape[1:]
    part, half = tok // 2, width // 2
    panels, _, rank_width = adapter_down_panels.shape[1:]
    vcols = adapter_up_panels.shape[3]
    qcols = encoded_query_rows.shape[2]
    chip_rows = width // n
    pads = [i * chip_rows % LANES for i in range(n)]
    win = -(-(max(pads) + chip_rows) // LANES) * LANES
    total = n * tok
    dma = pltpu.SemaphoreType.DMA
    any_spec = pl.BlockSpec(memory_space=pl.ANY)
    return pl.pallas_call(
        functools.partial(kernel, n),
        out_shape=jax.ShapeDtypeStruct(encoded_query_rows.shape, bf16),
        in_specs=[any_spec] * 11,
        out_specs=any_spec,
        scratch_shapes=[
            pltpu.SMEM(request_token_lengths.shape, jnp.int32),
            pltpu.SMEM(adapter_per_request.shape, jnp.int32),
            pltpu.SMEM(rank_per_adapter.shape, jnp.int32),
            pltpu.SMEM(slot_per_adapter.shape, jnp.int32),
            pltpu.VMEM((part, width), bf16),
            pltpu.VMEM((1, width), f32),
            pltpu.VMEM((n, part, width), bf16),
            pltpu.VMEM((win, 2 * vcols), bf16),
            pltpu.VMEM((panels, rank_width, width), bf16),
            pltpu.VMEM((panels, rank_width, half), bf16),
            pltpu.VMEM((width, 2 * panels * rank_width), bf16),
            pltpu.VMEM((2 * panels, rank_width, 2 * vcols), bf16),
            pltpu.VMEM((tok, qcols), bf16),
            pltpu.VMEM((n, tok, vcols), bf16),
            pltpu.VMEM((n, part, 2 * vcols), f32),
            pltpu.VMEM((n, part, 2 * vcols), bf16),
            pltpu.VMEM((n, part, 2 * vcols), bf16),
            pltpu.VMEM((n, part, 2 * vcols), bf16),
            pltpu.VMEM((n, part, 2 * vcols), bf16),
            pltpu.VMEM((n, part, 2 * vcols), bf16),
            pltpu.VMEM((n, 2, part, vcols), bf16),
            pltpu.VMEM((qcols // HEAD_SIZE, tok, total), bf16),
            pltpu.VMEM((tok, qcols), bf16),
            dma((11,)),
            dma((2,)),
            dma((10,)),
            dma((3,)),
            dma((3,)),
            dma((2,)),
            dma((4,)),
            dma((2,)),
            dma((4,)),
            dma,
            dma,
            dma,
            dma((3,)),
            dma,
            dma((n,)),
            dma((2,)),
            dma((n,)),
        ],
        compiler_params=pltpu.CompilerParams(
            collective_id=0, has_side_effects=True, vmem_limit_bytes=56 * 1024 * 1024
        ),
    )(
        layer_input_rows,
        encoded_query_rows,
        encoded_key_rows,
        layer_norm_gain,
        base_value_matrix,
        jnp.swapaxes(adapter_down_panels, 2, 3),
        adapter_up_panels,
        request_token_lengths,
        adapter_per_request,
        rank_per_adapter,
        slot_per_adapter,
    )


def solution(mesh):
    in_specs = (
        P("segment", ("groups", "seq"), None),
        P("segment", ("groups", "seq"), "owner"),
        P("segment", ("groups", "seq"), "owner"),
        P("segment", None),
        P("segment", ("seq", "owner"), None),
        P("segment", "seq", "owner", None),
        P("segment", "seq", None, "owner"),
        P("groups"),
        P("groups"),
        P(),
        P(),
    )
    out_specs = P("segment", ("groups", "seq"), "owner")
    n = mesh.shape["seq"]
    small = mesh.shape["owner"] == 2 and mesh.shape["groups"] == 2 and n == 4
    return jax.shard_map(
        functools.partial(fused, n) if small else per_device, mesh=mesh, in_specs=in_specs, out_specs=out_specs, check_vma=False
    )
```

time: 42.4 us -> 36.4 us (0.86); the launches traced: 42.3 us -> 35.7 us
  Pallas kernels: 40.7 us -> 34.2 us
    pallas_call x1, Pallas kernels: 40.7 us -> 34.2 us  [fused(): pl.pallas_call(functools.partial(kernel, n), out_shape=jax.ShapeDtypeStru...]
where the time goes in v2:
time: 36.4 us; the launch traced here: 35.7 us
  Pallas kernels  34.2 us (94%)
  local copies, waits for them, and re-layouts  1.57 us (4%)
    pallas_call x1, Pallas kernels, fused(): pl.pallas_call(functools.partial(kernel, n), out_shape=jax.ShapeDtypeStru...  34.2 us
    unnamed x1, local copies, waits for them, and re-layouts  1.57 us

profile of v2, /device:TPU:25, one launch (start us, length us, event | category | flops | bytes accessed | tf_op | source)
XLA Modules:
  0.0 35.7 jit_solution(7862980179736125451)
XLA Ops:
  0.0 34.2 %shard_map.109 = bf16[1,64,1024]{2,1,0:T(8,128)(2,1)} custom-call(bf16[1,64,5376]{2,1,0:T(8,128)(2,1)} %x_hbm.1, bf16[1,64,1024]{2,1,0:T(8,128)(2,1)} %q_hbm.1, bf16[1,64,512]{2,1,0:T(8,128)(2,1)} %k_hbm.1, f32[1,5376]{1,0:T(1,128)} %gain_hbm.1, bf16[1,672,1024]{2,1,0:T(8,128)(2,1)} %w_hbm.1, bf16[1,2,64,2688]{3,2,1,0:T(8,128)(2,1)} %bitcast.1, ...), custom_call_target="tpu_custom_call" | custom-call | tf_op jit(solution)/shard_map/pallas_call | solution.py:790
  34.2 1.6 %copy.13 = bf16[1,64,1024]{2,1,0:T(8,128)(2,1)} copy(bf16[1,64,1024]{2,1,0:T(8,128)(2,1)} %shard_map.109) | data formatting | bytes 262144

commit v3 on v2

--- a/solution.py
+++ b/solution.py
@@ -170,7 +170,7 @@
     adapters_hbm,
     ranks_hbm,
     slots_hbm,
-    out_hbm,
+    out,
     lengths,
     adapters,
     ranks,
@@ -191,9 +191,10 @@
     sbuf,
     srec,
     vbuf,
+    vx,
     vall,
+    va,
     prob,
-    ob,
     loc_sem,
     x_send,
     x_recv,
@@ -211,6 +212,8 @@
     s_recv,
     v_send,
     v_recv,
+    d_recv,
+    ready,
 ):
     f32, bf16 = jnp.float32, jnp.bfloat16
     s = lax.axis_index("seq")
@@ -316,23 +319,22 @@
     def rows_of(first, count, columns):
         return xb[first : first + count, :, columns].reshape(count * part, columns.size)
 
-    def partial(c, first, count, own, hosted, chip):
+    def own_partial(c, first, count, columns):
         slot_t, rank_t = token_facts(first, count)
         at, _ = window_of(c)
         base = dot(rows_of(first, count, pl.ds(at, win)), wbuf[...])
-        if hosted is None:
-            low = dot(rows_of(first, count, half_at(own)), dnt[half_at(own), :low_width])
-            low = masked(low, slot_t, rank_t, c)
-            raised = dot(low, ucat[:panels].reshape(low_width, vcols2))
-        else:
-            both = dot(rows_of(first, count, half_at(hosted)), dnt[half_at(hosted), :])
-            low = both[:, :low_width] + dot(rows_of(first, count, half_at(own)), dnt[half_at(own), :low_width])
-            low = jnp.concatenate(
-                [masked(low, slot_t, rank_t, c), masked(both[:, low_width:], slot_t, rank_t, chip)], axis=1
-            )
-            raised = dot(low, ucat[...].reshape(2 * low_width, vcols2))
+        low = dot(rows_of(first, count, columns), dnt[columns, :low_width])
+        raised = dot(masked(low, slot_t, rank_t, c), ucat[:panels].reshape(low_width, vcols2))
         value = base + raised * (adapter_strength / rank_t.astype(f32))
         return value.reshape(count, part, vcols2)
+
+    def hosted_partial(first, count, chip, columns):
+        slot_t, rank_t = token_facts(first, count)
+        low = dot(rows_of(first, count, columns), dnt[columns, low_width:])
+        raised = dot(masked(low, slot_t, rank_t, chip), ucat[panels:].reshape(low_width, vcols2))
+        value = raised * (adapter_strength / rank_t.astype(f32))
+        at = pl.ds(first, count)
+        pown[at] = pown[at] + value.reshape(count, part, vcols2)
 
     def chunk(q, up):
         at = (up if q < CHUNKS // 2 else 1 - up) * half + (q % 2) * wide
@@ -418,16 +420,13 @@
             soft = weights / jnp.sum(weights, axis=1, keepdims=True)
             prob[h] = soft.astype(bf16)
 
-    result = pltpu.make_async_copy(ob, out_hbm.at[0], loc_sem.at[0])
-
     def mix(c):
         values = vall[...].reshape(total, vcols)
         for h in range(q_heads):
             kv = h // group
-            ob[:, h * HEAD_SIZE : (h + 1) * HEAD_SIZE] = dot(
+            out[:, h * HEAD_SIZE : (h + 1) * HEAD_SIZE] = dot(
                 prob[h], values[:, kv * HEAD_SIZE : (kv + 1) * HEAD_SIZE]
             ).astype(bf16)
-        result.start()
 
     per_group = panels // 2
     mine = pl.ds(g * per_group, per_group)
@@ -451,7 +450,7 @@
         return remote(at, at, x_send.at[1], x_recv.at[index], peer(to))
 
     def k_up(c, t):
-        return remote(kb.at[t], kb.at[t], k_send, k_recv, peer(c + 1))
+        return remote(kb.at[t], kb.at[t], k_send, k_recv.at[t if c == 1 else 0], peer(c + 1))
 
     def end_program(c):
         low = c < n // 2
@@ -459,7 +458,10 @@
         inward = int(low)
         kept = 1 - inward
         host_core = inward
-        opening(c, [peer(c, other), peer(i), peer(i, other)], 3)
+        greetings = [peer(c, other), peer(i), peer(i, other)]
+        if low:
+            greetings += [peer(j), peer(j, other)]
+        opening(c, greetings, 3 if low else 5)
         w_copy, dn_copy, up_copy = exchange(c, kept)
         piece_in = remote(
             down_hbm.at[0, mine, other_piece, :], hdn.at[mine, other_piece, :], ph_send.at[1], ph_recv.at[1], peer(c, other)
@@ -472,17 +474,20 @@
         )
         up_z = remote(up_hbm.at[0, mine], ucat.at[my_up, :, my_cols], uh_send.at[0], uh_recv.at[0], peer(i))
 
+        if not low:
+            for core in (o, other):
+                pl.semaphore_signal(ready, inc=1, device_id=peer(j, core), device_id_type=pl.DeviceIdType.MESH)
+        before = 2 if low else 1
+        for q in range(before):
+            x_end(c, c, q, inward, i).start()
+
         @pl.when(o == host_core)
         def _():
             piece_in.start()
             piece_z.start()
-            up_z.start()
-            x_end(c, c, 0, inward, i).start()
 
         @pl.when(o != host_core)
         def _():
-            up_z.start()
-            x_end(c, c, 0, inward, i).start()
             dn_copy.start()
 
         w_copy.start()
@@ -493,11 +498,15 @@
             arrived(hdn.at[mine, my_piece, :], ph_recv.at[1])
             piece_on.start()
 
-        for q in range(1, CHUNKS):
-            x_end(c, c, q, inward, i).start()
+        if low:
+            x_end(c, c, before, inward, i).start()
+            before += 1
+        up_z.start()
         if c == 0:
             local[6].wait()
             k_up(c, c).start()
+        for q in range(before, CHUNKS):
+            x_end(c, c, q, inward, i).start()
         for at in (2, 3, 4):
             local[at].wait()
         read_tables()
@@ -511,41 +520,49 @@
         arrived(wbuf.at[pl.ds(0, slab)], ex_recv.at[0])
 
         def p_copy(t):
-            index = 1 if t == f else 2 if t == i and not low else 0
-            return remote(pbuf.at[t], prec.at[t], p_send, p_recv.at[index], peer(i))
-
-        p_core = remote(
-            pbuf.at[c, :, other_cols], prec.at[c, :, pl.ds(0, vcols)], s_send, s_recv.at[0], peer(c, other)
-        )
+            return remote(pbuf.at[t], prec.at[t], p_send.at[0], p_recv.at[t], peer(i))
+
+        def p_core(t):
+            return remote(
+                pbuf.at[t, :, other_cols], prec.at[t, :, pl.ds(0, vcols)], p_send.at[1], s_recv.at[t], peer(c, other)
+            )
 
         def end_partial(t):
-            pbuf[t] = partial(c, t, 1, kept, None, c)[0].astype(bf16)
+            pbuf[t] = own_partial(c, t, 1, half_at(kept))[0].astype(bf16)
+            if t == c or not low:
+                p_core(t).start()
 
         end_partial(c)
         if low:
             p_copy(c).start()
-        else:
-            p_core.start()
         for index, t in enumerate((i, j, f)):
             arrived(xb.at[t, :, half_at(kept)], x_recv.at[index])
             end_partial(t)
-            if low or t != i:
+            if low:
                 p_copy(t).start()
-            if not low and t == f:
-                p_copy(i).start()
+        if not low:
+            for t in range(c):
+                p_copy(t).start()
         local[5].wait()
-        if low:
-            attend(c)
-            arrived(vall.at[0], v_recv.at[0])
-        else:
+        if not low:
             local[6].wait()
-            arrived(kb.at[pl.ds(0, n - 1)], k_recv)
-            attend(c)
-            arrived(prec.at[c, :, pl.ds(0, vcols)], s_recv.at[0])
-            for t in range(n):
-                arrived(vall.at[t], v_recv.at[t])
-            vall[c, o] = (vall[c, o].astype(f32) + pbuf[c, :, my_cols].astype(f32)).astype(bf16)
-            vall[c, other] = (vall[c, other].astype(f32) + prec[c, :, 0:vcols].astype(f32)).astype(bf16)
+            arrived(kb.at[pl.ds(0, n - 1)], k_recv.at[0])
+        attend(c)
+
+        def take(t):
+            arrived(prec.at[t, :, pl.ds(0, vcols)], s_recv.at[t])
+            arrived(vall.at[t], v_recv.at[t])
+            own_rows = vall[t, o].astype(f32) + pbuf[t, :, my_cols].astype(f32)
+            other_rows = vall[t, other].astype(f32) + prec[t, :, 0:vcols].astype(f32)
+            if t == c:
+                arrived(va, d_recv)
+                own_rows = own_rows + va[o].astype(f32)
+                other_rows = other_rows + va[other].astype(f32)
+            vall[t, o] = own_rows.astype(bf16)
+            vall[t, other] = other_rows.astype(bf16)
+
+        for t in range(c + 1):
+            take(t)
         mix(c)
 
         sent(wbuf.at[pl.ds(0, slab)], ex_send.at[0])
@@ -564,11 +581,11 @@
         sent(xb.at[0], x_send.at[0])
         if c == 0:
             sent(kb.at[0], k_send)
-            sent(pbuf, p_send)
+            sent(pbuf, p_send.at[0])
+            sent(pbuf.at[0, :, other_cols], p_send.at[1])
         else:
-            sent(pbuf.at[pl.ds(0, n - 1)], p_send)
-            sent(pbuf.at[c, :, other_cols], s_send)
-        result.wait()
+            sent(pbuf.at[pl.ds(0, n - 1)], p_send.at[0])
+            sent(pbuf.at[:, :, other_cols], p_send.at[1])
 
     def inner_program(c):
         low = c < n // 2
@@ -576,24 +593,28 @@
         inward = int(low)
         outward = 1 - inward
         first = min(c, e, j)
-        opening(c, [peer(c, other), peer(e), peer(e, other), peer(j), peer(c, o, 1 - g)], 5)
+        greetings = [peer(c, other), peer(e), peer(e, other), peer(j), peer(c, o, 1 - g)]
+        if low:
+            greetings += [peer(f), peer(f, other)]
+        opening(c, greetings, 5 if low else 7)
         w_copy, dn_copy, up_copy = exchange(c, None)
-        for q in range(CHUNKS):
+
+        def own_across(q):
             x_across(c, q, inward, j, False).start()
-            if q < CHUNKS // 2:
-                x_outward(c, q, outward, e, 0).start()
+
+        for q in range(CHUNKS // 2):
+            own_across(q)
+            x_outward(c, q, outward, e, 0).start()
+        if not low:
+            own_across(2)
+            own_across(3)
         w_copy.start()
         dn_copy.start()
         up_copy.start()
         local[6].wait()
-        if not low:
-            k_up(c, c).start()
         for at in (2, 3, 4):
             local[at].wait()
         read_tables()
-        arrived(dn.at[:, :, other_half], ex_recv.at[1])
-        transpose_panels(dn, outward, 0)
-        transpose_panels(dn, inward, 0)
 
         def next_e(q):
             arrived(xb.at[e, :, chunk(q, inward)], x_recv.at[q])
@@ -621,6 +642,8 @@
             arrived(piece(mine, my_piece), ph_recv.at[0])
             pass_on(mine, my_piece, 0, 1, peer(c, o, 1 - g)).start()
             pass_on(mine, my_piece, 1, 2, peer(c, other)).start()
+
+        def host_up():
             arrived(ucat.at[my_up, :, my_cols], uh_recv.at[0])
             pass_up(my_up, 0, 1, peer(c, o, 1 - g)).start()
             pass_up(my_up, 1, 2, peer(c, other)).start()
@@ -638,93 +661,144 @@
             arrived(ucat.at[my_up, :, other_cols], uh_recv.at[2])
             arrived(ucat.at[their_up, :, other_cols], uh_recv.at[3])
 
+        def own_weights():
+            arrived(dn.at[:, :, other_half], ex_recv.at[1])
+            transpose_panels(dn, outward, 0)
+            transpose_panels(dn, inward, 0)
+            arrived(ucat.at[pl.ds(0, panels), :, other_cols], ex_recv.at[2])
+            arrived(wbuf.at[pl.ds(0, slab)], ex_recv.at[0])
+
+        def rest_of_j():
+            arrived(xb.at[j, :, half_at(inward)], x_recv.at[6])
+
+        def rest_of_f():
+            arrived(xb.at[f, :, half_at(inward)], x_recv.at[9])
+
+        def own(at, count):
+            pown[at : at + count] = own_partial(c, at, count, pl.ds(0, width))
+
+        def hosted(at, count):
+            hosted_partial(at, count, e, half_at(inward))
+
+        def s_copy(t):
+            return remote(sbuf.at[t], srec.at[t], s_send, s_recv.at[t], peer(j))
+
+        def s_far(t, core):
+            cols = pl.ds(core * vcols, vcols)
+            return remote(sbuf.at[t, :, cols], va.at[o], s_send, d_recv, peer(f, core))
+
+        def v_end(t, core):
+            cols = pl.ds(core * vcols, vcols)
+            return remote(vbuf.at[t, :, cols], vall.at[t, o], v_send.at[0], v_recv.at[t], peer(e, core))
+
+        def v_core(t):
+            return remote(vx.at[t, :, other_cols], vall.at[t, o], v_send.at[1], v_recv.at[t], peer(c, other))
+
+        def give_end(t):
+            v_end(t, 0).start()
+            v_end(t, 1).start()
+
+        def keep(t, value):
+            vx[t] = value.astype(bf16)
+            v_core(t).start()
+            vall[t, o] = vx[t, :, my_cols]
+
+        def early(t):
+            vbuf[t] = pown[t].astype(bf16)
+            give_end(t)
+
+        def add_end(t):
+            arrived(prec.at[t], p_recv.at[t])
+            value = pown[t] + prec[t].astype(f32)
+            sbuf[t] = value.astype(bf16)
+            if t == f:
+                if low:
+                    pl.semaphore_wait(ready, 2)
+                s_far(t, 0).start()
+                s_far(t, 1).start()
+            if t != f or not low:
+                s_copy(t).start()
+            return value
+
+        def relay(t):
+            arrived(srec.at[t], s_recv.at[t])
+            value = pown[t] + srec[t].astype(f32)
+            vbuf[t] = value.astype(bf16)
+            give_end(t)
+            if t == c:
+                arrived(prec.at[t], p_recv.at[t])
+            keep(t, value + prec[t].astype(f32))
+
+        def next_k(t):
+            arrived(kb.at[t], k_recv.at[t])
+            k_up(c, t).start()
+
         if low:
-            host_z()
-            next_j(0)
             next_e(0)
-            next_j(1)
             next_e(1)
-            host_y()
-            next_e(2)
-            next_e(3)
             k_up(c, c).start()
-            arrived(kb.at[0], k_recv)
-            k_up(c, 0).start()
-            host_done()
-            next_f(0)
-        else:
+            own_across(2)
+            own_weights()
             next_j(0)
             next_j(1)
             host_z()
+            rest_of_j()
+            next_e(2)
+            own_across(3)
+            host_up()
+            next_f(0)
+            next_k(0)
+            next_e(3)
+            own(first, 3)
+            next_f(1)
+            host_y()
+            host_done()
+            hosted(first, 3)
+            early(e)
+            for t in range(3):
+                pown[t] = add_end(t)
+            local[5].wait()
+            attend(c)
+            rest_of_f()
+            own(f, 1)
+            hosted(f, 1)
+            add_end(f)
+            for t in (1, 0):
+                arrived(srec.at[t], s_recv.at[t])
+                keep(t, pown[t] + srec[t].astype(f32))
+        else:
+            own_weights()
+            next_j(0)
+            next_j(1)
             next_e(0)
             next_f(0)
+            next_f(1)
+            k_up(c, c).start()
+            host_z()
+            host_up()
             next_e(1)
+            next_k(1)
+            next_e(2)
+            next_e(3)
             host_y()
-            next_f(1)
-            next_e(2)
+            own(c, 2)
             host_done()
-            next_e(3)
-        arrived(ucat.at[pl.ds(0, panels), :, other_cols], ex_recv.at[2])
-        arrived(wbuf.at[pl.ds(0, slab)], ex_recv.at[0])
-        arrived(xb.at[j, :, half_at(inward)], x_recv.at[6])
-        pown[first : first + 3] = partial(c, first, 3, outward, inward, e)
-        if low:
-            next_f(1)
-
-        def s_copy(t):
-            return remote(sbuf.at[t], srec.at[t], s_send, s_recv.at[t], peer(j))
-
-        def add_end(t):
-            if low or t != e:
-                value = pown[t] + prec[t].astype(f32)
-                pown[t] = value
-                if low or t < n // 2:
-                    sbuf[t] = value.astype(bf16)
-                    s_copy(t).start()
-
-        if low:
-            arrived(prec.at[pl.ds(0, 3)], p_recv.at[0])
-            for t in range(3):
-                add_end(t)
-        arrived(xb.at[f, :, half_at(inward)], x_recv.at[9])
-        pown[f] = partial(c, f, 1, outward, inward, e)[0]
-        if not low:
-            arrived(prec.at[j], p_recv.at[0])
+            hosted(c, 2)
+            early(e)
+            next_k(0)
+            rest_of_f()
+            own(f, 1)
+            hosted(f, 1)
+            add_end(f)
+            relay(f)
+            rest_of_j()
+            own(j, 1)
+            hosted(j, 1)
             add_end(j)
-        arrived(prec.at[f], p_recv.at[1])
-        add_end(f)
-        local[5].wait()
-        if not low:
-            arrived(kb.at[pl.ds(0, 2)], k_recv)
-            for t in range(2):
-                k_up(c, t).start()
-        attend(c)
-
-        def v_end(t, core):
-            cols = pl.ds(core * vcols, vcols)
-            return remote(vbuf.at[t, :, cols], vall.at[t, o], v_send.at[0], v_recv.at[t], peer(e, core))
-
-        def v_core(t):
-            return remote(vbuf.at[t, :, other_cols], vall.at[t, o], v_send.at[1], v_recv.at[t], peer(c, other))
-
-        def finish(t):
-            arrived(srec.at[t], s_recv.at[t])
-            vbuf[t] = (pown[t] + srec[t].astype(f32)).astype(bf16)
-            if t == 0 or not low:
-                v_end(t, 0).start()
-                v_end(t, 1).start()
-            if t <= c:
-                v_core(t).start()
-                vall[t, o] = vbuf[t, :, my_cols]
-
-        if low:
-            finish(1)
-            finish(0)
-        else:
-            arrived(prec.at[c], p_recv.at[2])
-            pown[c] = pown[c] + prec[c].astype(f32)
-            for t in range(n):
-                finish(t)
+            relay(j)
+            relay(c)
+            local[5].wait()
+            attend(c)
         for t in range(c + 1):
             arrived(vall.at[t, other], v_recv.at[t])
         mix(c)
@@ -743,10 +817,9 @@
             sent(sbuf, s_send)
             sent(vbuf.at[0], v_send.at[0])
         else:
-            sent(sbuf.at[pl.ds(0, 2)], s_send)
+            sent(sbuf.at[pl.ds(0, 3)], s_send)
             sent(vbuf, v_send.at[0])
-        sent(vbuf.at[pl.ds(0, c + 1), :, pl.ds(0, vcols)], v_send.at[1])
-        result.wait()
+        sent(vx.at[pl.ds(0, c + 1), :, pl.ds(0, vcols)], v_send.at[1])
 
     for c in range(n):
 
@@ -789,9 +862,9 @@
     any_spec = pl.BlockSpec(memory_space=pl.ANY)
     return pl.pallas_call(
         functools.partial(kernel, n),
-        out_shape=jax.ShapeDtypeStruct(encoded_query_rows.shape, bf16),
+        out_shape=pltpu.VMEM(encoded_query_rows.shape[1:], bf16),
         in_specs=[any_spec] * 11,
-        out_specs=any_spec,
+        out_specs=pl.BlockSpec(memory_space=pltpu.VMEM),
         scratch_shapes=[
             pltpu.SMEM(request_token_lengths.shape, jnp.int32),
             pltpu.SMEM(adapter_per_request.shape, jnp.int32),
@@ -813,9 +886,10 @@
             pltpu.VMEM((n, part, 2 * vcols), bf16),
             pltpu.VMEM((n, part, 2 * vcols), bf16),
             pltpu.VMEM((n, part, 2 * vcols), bf16),
+            pltpu.VMEM((n, part, 2 * vcols), bf16),
             pltpu.VMEM((n, 2, part, vcols), bf16),
+            pltpu.VMEM((2, part, vcols), bf16),
             pltpu.VMEM((qcols // HEAD_SIZE, tok, total), bf16),
-            pltpu.VMEM((tok, qcols), bf16),
             dma((11,)),
             dma((2,)),
             dma((10,)),
@@ -826,13 +900,15 @@
             dma((2,)),
             dma((4,)),
             dma,
-            dma,
-            dma,
-            dma((3,)),
+            dma((2,)),
+            dma((2,)),
+            dma((n,)),
             dma,
             dma((n,)),
             dma((2,)),
             dma((n,)),
+            dma,
+            pltpu.SemaphoreType.REGULAR,
         ],
         compiler_params=pltpu.CompilerParams(
             collective_id=0, has_side_effects=True, vmem_limit_bytes=56 * 1024 * 1024
@@ -849,7 +925,7 @@
         adapter_per_request,
         rank_per_adapter,
         slot_per_adapter,
-    )
+    )[None]
 
 
 def solution(mesh):

time: 36.4 us -> 31.2 us (0.86); the launches traced: 35.7 us -> 31.1 us
  Pallas kernels: 34.2 us -> 30.4 us
  local copies, waits for them, and re-layouts: 1.57 us -> 0.66 us
    pallas_call x1, Pallas kernels: 34.2 us -> 30.4 us  [fused(): pl.pallas_call(functools.partial(kernel, n), out_shape=pltpu.VMEM(encoded...]
    unnamed x1, local copies, waits for them, and re-layouts: 1.57 us -> 0.66 us
where the time goes in v3:
time: 31.2 us; the launch traced here: 31.1 us
  Pallas kernels  30.4 us (97%)
  local copies, waits for them, and re-layouts  0.66 us (2%)
    pallas_call x1, Pallas kernels, fused(): pl.pallas_call(functools.partial(kernel, n), out_shape=pltpu.VMEM(encoded...  30.4 us
    unnamed x1, local copies, waits for them, and re-layouts  0.66 us

profile of v3, /device:TPU:25, one launch (start us, length us, event | category | flops | bytes accessed | tf_op | source)
XLA Modules:
  0.0 31.1 jit_solution(16657764156873347842)
XLA Ops:
  0.0 30.4 %shard_map.109 = bf16[64,1024]{1,0:T(8,128)(2,1)S(1)} custom-call(bf16[1,64,5376]{2,1,0:T(8,128)(2,1)} %x_hbm.1, bf16[1,64,1024]{2,1,0:T(8,128)(2,1)} %q_hbm.1, bf16[1,64,512]{2,1,0:T(8,128)(2,1)} %k_hbm.1, f32[1,5376]{1,0:T(1,128)} %gain_hbm.1, bf16[1,672,1024]{2,1,0:T(8,128)(2,1)} %w_hbm.1, bf16[1,2,64,2688]{3,2,1,0:T(8,128)(2,1)} %bitcast.3, ...), custom_call_target="tpu_custom_call" | custom-call | tf_op jit(solution)/shard_map/pallas_call | solution.py:863
  30.4 0.7 %copy.13 = bf16[1,64,1024]{2,1,0:T(8,128)(2,1)} copy(bf16[1,64,1024]{2,1,0:T(8,128)(2,1)S(1)} %bitcast.2) | data formatting | bytes 262144

commit v4 on v3

--- a/solution.py
+++ b/solution.py
@@ -186,6 +186,7 @@
     qb,
     kb,
     pown,
+    lowa,
     pbuf,
     prec,
     sbuf,
@@ -213,6 +214,7 @@
     v_send,
     v_recv,
     d_recv,
+    d_send,
     ready,
 ):
     f32, bf16 = jnp.float32, jnp.bfloat16
@@ -319,22 +321,39 @@
     def rows_of(first, count, columns):
         return xb[first : first + count, :, columns].reshape(count * part, columns.size)
 
-    def own_partial(c, first, count, columns):
-        slot_t, rank_t = token_facts(first, count)
+    def end_value(c, t, columns):
+        slot_t, rank_t = token_facts(t, 1)
+        at, _ = window_of(c)
+        base = dot(xb[t, :, pl.ds(at, win)], wbuf[...])
+        low = masked(dot(xb[t, :, columns], dnt[columns, :low_width]), slot_t, rank_t, c)
+        raised = dot(low, ucat[:panels].reshape(low_width, vcols2))
+        return base + raised * (adapter_strength / rank_t.astype(f32))
+
+    def first_part(c, first, count, columns):
         at, _ = window_of(c)
         base = dot(rows_of(first, count, pl.ds(at, win)), wbuf[...])
         low = dot(rows_of(first, count, columns), dnt[columns, :low_width])
-        raised = dot(masked(low, slot_t, rank_t, c), ucat[:panels].reshape(low_width, vcols2))
-        value = base + raised * (adapter_strength / rank_t.astype(f32))
-        return value.reshape(count, part, vcols2)
-
-    def hosted_partial(first, count, chip, columns):
+        pown[pl.ds(first, count)] = base.reshape(count, part, vcols2)
+        lowa[pl.ds(first, count)] = low.reshape(count, part, low_width)
+
+    def last_part(c, first, count, chip, columns):
         slot_t, rank_t = token_facts(first, count)
-        low = dot(rows_of(first, count, columns), dnt[columns, low_width:])
-        raised = dot(masked(low, slot_t, rank_t, chip), ucat[panels:].reshape(low_width, vcols2))
+        at = pl.ds(first, count)
+        both = dot(rows_of(first, count, columns), dnt[columns, :])
+        low = lowa[at].reshape(count * part, low_width) + both[:, :low_width]
+        low = jnp.concatenate(
+            [masked(low, slot_t, rank_t, c), masked(both[:, low_width:], slot_t, rank_t, chip)], axis=1
+        )
+        raised = dot(low, ucat[...].reshape(2 * low_width, vcols2))
         value = raised * (adapter_strength / rank_t.astype(f32))
-        at = pl.ds(first, count)
         pown[at] = pown[at] + value.reshape(count, part, vcols2)
+
+    def put(ref, t, value):
+        for side in range(2):
+            ref[t, side] = value[:, side * vcols : (side + 1) * vcols].astype(bf16)
+
+    def get(ref, t):
+        return jnp.concatenate([ref[t, 0], ref[t, 1]], axis=1).astype(f32)
 
     def chunk(q, up):
         at = (up if q < CHUNKS // 2 else 1 - up) * half + (q % 2) * wide
@@ -478,16 +497,25 @@
             for core in (o, other):
                 pl.semaphore_signal(ready, inc=1, device_id=peer(j, core), device_id_type=pl.DeviceIdType.MESH)
         before = 2 if low else 1
-        for q in range(before):
-            x_end(c, c, q, inward, i).start()
+
+        def open_rows(opening_count=before):
+            for q in range(opening_count):
+                x_end(c, c, q, inward, i).start()
+
+        if low:
+            open_rows()
 
         @pl.when(o == host_core)
         def _():
             piece_in.start()
             piece_z.start()
+            if not low:
+                open_rows()
 
         @pl.when(o != host_core)
         def _():
+            if not low:
+                open_rows()
             dn_copy.start()
 
         w_copy.start()
@@ -524,11 +552,11 @@
 
         def p_core(t):
             return remote(
-                pbuf.at[t, :, other_cols], prec.at[t, :, pl.ds(0, vcols)], p_send.at[1], s_recv.at[t], peer(c, other)
+                pbuf.at[t, other], prec.at[t, 0], p_send.at[1], s_recv.at[t], peer(c, other)
             )
 
         def end_partial(t):
-            pbuf[t] = own_partial(c, t, 1, half_at(kept))[0].astype(bf16)
+            put(pbuf, t, end_value(c, t, half_at(kept)))
             if t == c or not low:
                 p_core(t).start()
 
@@ -550,14 +578,15 @@
         attend(c)
 
         def take(t):
-            arrived(prec.at[t, :, pl.ds(0, vcols)], s_recv.at[t])
+            arrived(prec.at[t, 0], s_recv.at[t])
             arrived(vall.at[t], v_recv.at[t])
-            own_rows = vall[t, o].astype(f32) + pbuf[t, :, my_cols].astype(f32)
-            other_rows = vall[t, other].astype(f32) + prec[t, :, 0:vcols].astype(f32)
-            if t == c:
-                arrived(va, d_recv)
-                own_rows = own_rows + va[o].astype(f32)
-                other_rows = other_rows + va[other].astype(f32)
+            own_rows = vall[t, o].astype(f32) + pbuf[t, o].astype(f32)
+            other_rows = vall[t, other].astype(f32) + prec[t, 0].astype(f32)
+            if t == c or t == i:
+                at = int(t != c)
+                arrived(va.at[at], d_recv.at[at])
+                own_rows = own_rows + va[at, o].astype(f32)
+                other_rows = other_rows + va[at, other].astype(f32)
             vall[t, o] = own_rows.astype(bf16)
             vall[t, other] = other_rows.astype(bf16)
 
@@ -582,10 +611,10 @@
         if c == 0:
             sent(kb.at[0], k_send)
             sent(pbuf, p_send.at[0])
-            sent(pbuf.at[0, :, other_cols], p_send.at[1])
+            sent(pbuf.at[0, 0], p_send.at[1])
         else:
             sent(pbuf.at[pl.ds(0, n - 1)], p_send.at[0])
-            sent(pbuf.at[:, :, other_cols], p_send.at[1])
+            sent(pbuf.at[:, 0], p_send.at[1])
 
     def inner_program(c):
         low = c < n // 2
@@ -651,6 +680,8 @@
         def host_y():
             arrived(piece(theirs, my_piece), ph_recv.at[1])
             pass_on(theirs, my_piece, 1, 3, peer(c, other)).start()
+
+        def host_yu():
             arrived(ucat.at[their_up, :, my_cols], uh_recv.at[1])
             pass_up(their_up, 1, 3, peer(c, other)).start()
 
@@ -675,44 +706,43 @@
             arrived(xb.at[f, :, half_at(inward)], x_recv.at[9])
 
         def own(at, count):
-            pown[at : at + count] = own_partial(c, at, count, pl.ds(0, width))
+            first_part(c, at, count, half_at(outward))
 
         def hosted(at, count):
-            hosted_partial(at, count, e, half_at(inward))
+            last_part(c, at, count, e, half_at(inward))
 
         def s_copy(t):
             return remote(sbuf.at[t], srec.at[t], s_send, s_recv.at[t], peer(j))
 
         def s_far(t, core):
-            cols = pl.ds(core * vcols, vcols)
-            return remote(sbuf.at[t, :, cols], va.at[o], s_send, d_recv, peer(f, core))
+            at = int(t != f)
+            return remote(sbuf.at[t, core], va.at[at, o], d_send, d_recv.at[at], peer(f, core))
 
         def v_end(t, core):
-            cols = pl.ds(core * vcols, vcols)
-            return remote(vbuf.at[t, :, cols], vall.at[t, o], v_send.at[0], v_recv.at[t], peer(e, core))
+            return remote(vbuf.at[t, core], vall.at[t, o], v_send.at[0], v_recv.at[t], peer(e, core))
 
         def v_core(t):
-            return remote(vx.at[t, :, other_cols], vall.at[t, o], v_send.at[1], v_recv.at[t], peer(c, other))
+            return remote(vx.at[t, other], vall.at[t, o], v_send.at[1], v_recv.at[t], peer(c, other))
 
         def give_end(t):
             v_end(t, 0).start()
             v_end(t, 1).start()
 
         def keep(t, value):
-            vx[t] = value.astype(bf16)
+            put(vx, t, value)
             v_core(t).start()
-            vall[t, o] = vx[t, :, my_cols]
+            vall[t, o] = vx[t, o]
 
         def early(t):
-            vbuf[t] = pown[t].astype(bf16)
+            put(vbuf, t, pown[t])
             give_end(t)
 
         def add_end(t):
             arrived(prec.at[t], p_recv.at[t])
-            value = pown[t] + prec[t].astype(f32)
-            sbuf[t] = value.astype(bf16)
-            if t == f:
-                if low:
+            value = pown[t] + get(prec, t)
+            put(sbuf, t, value)
+            if t == f or (low and t == j):
+                if low and t == j:
                     pl.semaphore_wait(ready, 2)
                 s_far(t, 0).start()
                 s_far(t, 1).start()
@@ -722,12 +752,13 @@
 
         def relay(t):
             arrived(srec.at[t], s_recv.at[t])
-            value = pown[t] + srec[t].astype(f32)
-            vbuf[t] = value.astype(bf16)
-            give_end(t)
+            value = pown[t] + get(srec, t)
             if t == c:
                 arrived(prec.at[t], p_recv.at[t])
-            keep(t, value + prec[t].astype(f32))
+            else:
+                put(vbuf, t, value)
+                give_end(t)
+            keep(t, value + get(prec, t))
 
         def next_k(t):
             arrived(kb.at[t], k_recv.at[t])
@@ -748,53 +779,55 @@
             host_up()
             next_f(0)
             next_k(0)
+            host_y()
             next_e(3)
+            host_yu()
+            next_f(1)
             own(first, 3)
-            next_f(1)
-            host_y()
             host_done()
             hosted(first, 3)
             early(e)
             for t in range(3):
                 pown[t] = add_end(t)
+            own(f, 1)
             local[5].wait()
             attend(c)
             rest_of_f()
-            own(f, 1)
             hosted(f, 1)
             add_end(f)
             for t in (1, 0):
                 arrived(srec.at[t], s_recv.at[t])
-                keep(t, pown[t] + srec[t].astype(f32))
+                keep(t, pown[t] + get(srec, t))
         else:
             own_weights()
             next_j(0)
             next_j(1)
+            host_z()
+            next_f(0)
             next_e(0)
-            next_f(0)
             next_f(1)
             k_up(c, c).start()
-            host_z()
             host_up()
+            next_k(1)
+            own(f, 2)
             next_e(1)
-            next_k(1)
+            host_y()
             next_e(2)
+            host_yu()
             next_e(3)
-            host_y()
             own(c, 2)
             host_done()
             hosted(c, 2)
+            early(c)
             early(e)
             next_k(0)
             rest_of_f()
-            own(f, 1)
             hosted(f, 1)
             add_end(f)
-            relay(f)
             rest_of_j()
-            own(j, 1)
             hosted(j, 1)
             add_end(j)
+            relay(f)
             relay(j)
             relay(c)
             local[5].wait()
@@ -814,12 +847,14 @@
         sent(ucat.at[pl.ds(panels, panels), :, my_cols], uh_send.at[1])
         sent(kb.at[pl.ds(0, c + 1)], k_send)
         if low:
-            sent(sbuf, s_send)
+            sent(sbuf.at[pl.ds(0, 3)], s_send)
+            sent(sbuf.at[pl.ds(0, 2)], d_send)
             sent(vbuf.at[0], v_send.at[0])
         else:
-            sent(sbuf.at[pl.ds(0, 3)], s_send)
+            sent(sbuf.at[pl.ds(0, 2)], s_send)
+            sent(sbuf.at[0], d_send)
             sent(vbuf, v_send.at[0])
-        sent(vx.at[pl.ds(0, c + 1), :, pl.ds(0, vcols)], v_send.at[1])
+        sent(vx.at[pl.ds(0, c + 1), 0], v_send.at[1])
 
     for c in range(n):
 
@@ -881,14 +916,15 @@
             pltpu.VMEM((tok, qcols), bf16),
             pltpu.VMEM((n, tok, vcols), bf16),
             pltpu.VMEM((n, part, 2 * vcols), f32),
-            pltpu.VMEM((n, part, 2 * vcols), bf16),
-            pltpu.VMEM((n, part, 2 * vcols), bf16),
-            pltpu.VMEM((n, part, 2 * vcols), bf16),
-            pltpu.VMEM((n, part, 2 * vcols), bf16),
-            pltpu.VMEM((n, part, 2 * vcols), bf16),
-            pltpu.VMEM((n, part, 2 * vcols), bf16),
+            pltpu.VMEM((n, part, panels * rank_width), f32),
             pltpu.VMEM((n, 2, part, vcols), bf16),
-            pltpu.VMEM((2, part, vcols), bf16),
+            pltpu.VMEM((n, 2, part, vcols), bf16),
+            pltpu.VMEM((n, 2, part, vcols), bf16),
+            pltpu.VMEM((n, 2, part, vcols), bf16),
+            pltpu.VMEM((n, 2, part, vcols), bf16),
+            pltpu.VMEM((n, 2, part, vcols), bf16),
+            pltpu.VMEM((n, 2, part, vcols), bf16),
+            pltpu.VMEM((2, 2, part, vcols), bf16),
             pltpu.VMEM((qcols // HEAD_SIZE, tok, total), bf16),
             dma((11,)),
             dma((2,)),
@@ -907,6 +943,7 @@
             dma((n,)),
             dma((2,)),
             dma((n,)),
+            dma((2,)),
             dma,
             pltpu.SemaphoreType.REGULAR,
         ],

time: 31.2 us -> 30.9 us (level)
  no operation moved by 1% of the time
where the time goes in v4:
time: 30.9 us; the launch traced here: 30.8 us
  Pallas kernels  30.1 us (97%)
  local copies, waits for them, and re-layouts  0.66 us (2%)
    pallas_call x1, Pallas kernels, fused(): pl.pallas_call(functools.partial(kernel, n), out_shape=pltpu.VMEM(encoded...  30.1 us
    unnamed x1, local copies, waits for them, and re-layouts  0.66 us

profile of v4, /device:TPU:25, one launch (start us, length us, event | category | flops | bytes accessed | tf_op | source)
XLA Modules:
  0.0 30.8 jit_solution(2551929005572385757)
XLA Ops:
  0.0 30.1 %shard_map.109 = bf16[64,1024]{1,0:T(8,128)(2,1)S(1)} custom-call(bf16[1,64,5376]{2,1,0:T(8,128)(2,1)} %x_hbm.1, bf16[1,64,1024]{2,1,0:T(8,128)(2,1)} %q_hbm.1, bf16[1,64,512]{2,1,0:T(8,128)(2,1)} %k_hbm.1, f32[1,5376]{1,0:T(1,128)} %gain_hbm.1, bf16[1,672,1024]{2,1,0:T(8,128)(2,1)} %w_hbm.1, bf16[1,2,64,2688]{3,2,1,0:T(8,128)(2,1)} %bitcast.3, ...), custom_call_target="tpu_custom_call" | custom-call | tf_op jit(solution)/shard_map/pallas_call | solution.py:898
  30.1 0.7 %copy.13 = bf16[1,64,1024]{2,1,0:T(8,128)(2,1)} copy(bf16[1,64,1024]{2,1,0:T(8,128)(2,1)S(1)} %bitcast.2) | data formatting | bytes 262144

commit v5 on v4

--- a/solution.py
+++ b/solution.py
@@ -384,7 +384,7 @@
                 low_width, half // 3
             ).T
 
-    def opening(c, greetings, count):
+    def opening(c, greetings, count, at_once=None):
         local[0].start()
         local[1].start()
         w_local = pltpu.make_async_copy(w_hbm.at[0], wbuf.at[slab_at(c)], loc_sem.at[2])
@@ -402,12 +402,16 @@
         for t in range(c + 1, n):
             kb[t] = jnp.zeros(kb.shape[1:], bf16)
             vall[t] = jnp.zeros(vall.shape[1:], bf16)
+        if at_once is not None:
+            pl.semaphore_wait(barrier, count)
+            at_once()
         local[0].wait()
         local[1].wait()
         rows = xr[...].astype(f32)
         inv = lax.rsqrt(jnp.mean(rows * rows, axis=1, keepdims=True) + norm_eps)
         xb[c] = (xr[...].astype(f32) * inv * gain[...]).astype(bf16)
-        pl.semaphore_wait(barrier, count)
+        if at_once is None:
+            pl.semaphore_wait(barrier, count)
 
     def exchange(c, kept):
         w_copy = remote(w_hbm.at[0], wbuf.at[slab_at(c)], ex_send.at[0], ex_recv.at[0], peer(c, other))
@@ -480,7 +484,6 @@
         greetings = [peer(c, other), peer(i), peer(i, other)]
         if low:
             greetings += [peer(j), peer(j, other)]
-        opening(c, greetings, 3 if low else 5)
         w_copy, dn_copy, up_copy = exchange(c, kept)
         piece_in = remote(
             down_hbm.at[0, mine, other_piece, :], hdn.at[mine, other_piece, :], ph_send.at[1], ph_recv.at[1], peer(c, other)
@@ -493,6 +496,21 @@
         )
         up_z = remote(up_hbm.at[0, mine], ucat.at[my_up, :, my_cols], uh_send.at[0], uh_recv.at[0], peer(i))
 
+        def panels_out():
+            @pl.when(o == host_core)
+            def _():
+                piece_in.start()
+                piece_z.start()
+
+            @pl.when(o != host_core)
+            def _():
+                dn_copy.start()
+
+            w_copy.start()
+            up_copy.start()
+
+        opening(c, greetings, 3 if low else 5, None if low else panels_out)
+
         if not low:
             for core in (o, other):
                 pl.semaphore_signal(ready, inc=1, device_id=peer(j, core), device_id_type=pl.DeviceIdType.MESH)
@@ -502,24 +520,9 @@
             for q in range(opening_count):
                 x_end(c, c, q, inward, i).start()
 
+        open_rows()
         if low:
-            open_rows()
-
-        @pl.when(o == host_core)
-        def _():
-            piece_in.start()
-            piece_z.start()
-            if not low:
-                open_rows()
-
-        @pl.when(o != host_core)
-        def _():
-            if not low:
-                open_rows()
-            dn_copy.start()
-
-        w_copy.start()
-        up_copy.start()
+            panels_out()
 
         @pl.when(o != host_core)
         def _():
@@ -590,7 +593,7 @@
             vall[t, o] = own_rows.astype(bf16)
             vall[t, other] = other_rows.astype(bf16)
 
-        for t in range(c + 1):
+        for t in (0,) if low else (0, i, c, j):
             take(t)
         mix(c)
 
@@ -829,9 +832,9 @@
             add_end(j)
             relay(f)
             relay(j)
-            relay(c)
             local[5].wait()
             attend(c)
+            relay(c)
         for t in range(c + 1):
             arrived(vall.at[t, other], v_recv.at[t])
         mix(c)

time: 30.9 us -> 30.9 us (level)
  no operation moved by 1% of the time
where the time goes in v5:
time: 30.9 us; the launch traced here: 30.7 us
  Pallas kernels  30.1 us (97%)
  local copies, waits for them, and re-layouts  0.66 us (2%)
    pallas_call x1, Pallas kernels, fused(): pl.pallas_call(functools.partial(kernel, n), out_shape=pltpu.VMEM(encoded...  30.1 us
    unnamed x1, local copies, waits for them, and re-layouts  0.66 us

profile of v5, /device:TPU:25, one launch (start us, length us, event | category | flops | bytes accessed | tf_op | source)
XLA Modules:
  0.0 30.7 jit_solution(9296188695671926056)
XLA Ops:
  0.0 30.1 %shard_map.109 = bf16[64,1024]{1,0:T(8,128)(2,1)S(1)} custom-call(bf16[1,64,5376]{2,1,0:T(8,128)(2,1)} %x_hbm.1, bf16[1,64,1024]{2,1,0:T(8,128)(2,1)} %q_hbm.1, bf16[1,64,512]{2,1,0:T(8,128)(2,1)} %k_hbm.1, f32[1,5376]{1,0:T(1,128)} %gain_hbm.1, bf16[1,672,1024]{2,1,0:T(8,128)(2,1)} %w_hbm.1, bf16[1,2,64,2688]{3,2,1,0:T(8,128)(2,1)} %bitcast.3, ...), custom_call_target="tpu_custom_call" | custom-call | tf_op jit(solution)/shard_map/pallas_call | solution.py:901
  30.1 0.7 %copy.13 = bf16[1,64,1024]{2,1,0:T(8,128)(2,1)} copy(bf16[1,64,1024]{2,1,0:T(8,128)(2,1)S(1)} %bitcast.2) | data formatting | bytes 262144

commit v6 on v5

--- a/solution.py
+++ b/solution.py
@@ -728,8 +728,8 @@
             return remote(vx.at[t, other], vall.at[t, o], v_send.at[1], v_recv.at[t], peer(c, other))
 
         def give_end(t):
-            v_end(t, 0).start()
-            v_end(t, 1).start()
+            v_end(t, o).start()
+            v_end(t, other).start()
 
         def keep(t, value):
             put(vx, t, value)

time: 30.9 us -> 30.9 us (level)
  no operation moved by 1% of the time
where the time goes in v6:
time: 30.9 us; the launch traced here: 30.7 us
  Pallas kernels  30.1 us (97%)
  local copies, waits for them, and re-layouts  0.66 us (2%)
    pallas_call x1, Pallas kernels, fused(): pl.pallas_call(functools.partial(kernel, n), out_shape=pltpu.VMEM(encoded...  30.1 us
    unnamed x1, local copies, waits for them, and re-layouts  0.66 us

profile of v6, /device:TPU:25, one launch (start us, length us, event | category | flops | bytes accessed | tf_op | source)
XLA Modules:
  0.0 30.7 jit_solution(12075703943366191622)
XLA Ops:
  0.0 30.1 %shard_map.109 = bf16[64,1024]{1,0:T(8,128)(2,1)S(1)} custom-call(bf16[1,64,5376]{2,1,0:T(8,128)(2,1)} %x_hbm.1, bf16[1,64,1024]{2,1,0:T(8,128)(2,1)} %q_hbm.1, bf16[1,64,512]{2,1,0:T(8,128)(2,1)} %k_hbm.1, f32[1,5376]{1,0:T(1,128)} %gain_hbm.1, bf16[1,672,1024]{2,1,0:T(8,128)(2,1)} %w_hbm.1, bf16[1,2,64,2688]{3,2,1,0:T(8,128)(2,1)} %bitcast.3, ...), custom_call_target="tpu_custom_call" | custom-call | tf_op jit(solution)/shard_map/pallas_call | solution.py:901
  30.1 0.7 %copy.13 = bf16[1,64,1024]{2,1,0:T(8,128)(2,1)} copy(bf16[1,64,1024]{2,1,0:T(8,128)(2,1)S(1)} %bitcast.2) | data formatting | bytes 262144
